TPU v7x, 512 devices: a whole 4x4x16 slice. The times are simulated.
512 devices in a mesh: pair: 64 (over z, y_hi, core), rows: 8 (over x, y_lo).
Axes of the slice: x: 4, y: 4 (y_hi: 2, y_lo: 2; y = y_hi * 2 + y_lo), z: 16, core: 2. Of those that a mesh axis runs over, the one named last changes fastest.
Arguments:
- snapshot: float32 [1536, 32768], P('rows', 'pair'), may hold values from -40 to 40
- keep_side: int32 [2, 64], P(None, 'pair'), may hold values 0 or 1
Outputs:
- rotated: float32 [1536, 32768], P('rows', 'pair')
All inputs are finite; a program needn't handle non-finite values. No bound on the sum of `keep_side` on one device may be relied on, other than what follows from the above.
Results may differ from a plain program's by a relative error of at most 0.00013.
Values sent between devices are 32-bit elements; how exact they have to be, the bound alone decides.
No kernel may reach another device: no remote copies, remote signals or barrier semaphores. Data moves between devices by JAX's collectives and lax.ppermute only.
A program may use at most 64 MiB of HBM per device.

v0:
```python
import jax
import jax.numpy as jnp
from jax import lax
from jax.sharding import PartitionSpec as P

ROUNDS = 2


EPS = 1e-06


def shifted(value, axis, steps):
    count = lax.axis_size(axis)
    pairs = [(source, (source + steps) % count) for source in range(count)]
    return lax.ppermute(value, axis, pairs)


def polar_map(gram, total_rows):
    high = lax.Precision.HIGHEST
    width = gram.shape[0]
    diag_vals = jnp.diagonal(gram)
    inv_norm = lax.rsqrt(diag_vals / total_rows + EPS)
    corr = gram * inv_norm[:, None] * inv_norm[None, :] / total_rows
    scale = jnp.sqrt(jnp.sum(corr * corr) / width)
    e_mat = corr / scale
    eye = jnp.eye(width, dtype=jnp.float32)
    e_two = jnp.dot(e_mat, e_mat, precision=high)
    b_one = (9.0 * e_mat - 6.0 * e_two + jnp.dot(e_mat, e_two, precision=high)) * 0.25
    t_zero = (3.0 * eye - e_mat) * 0.5
    t_one = (3.0 * eye - b_one) * 0.5
    z_two = jnp.dot(t_zero, t_one, precision=high)
    b_two = jnp.dot(jnp.dot(b_one, t_one, precision=high), t_one, precision=high)
    t_two = (3.0 * eye - b_two) * 0.5
    z_three = jnp.dot(z_two, t_two, precision=high)
    return z_three * (inv_norm / jnp.sqrt(scale))[:, None]


def assemble(upper_left, corner, lower_right):
    upper = jnp.concatenate([upper_left, corner], axis=1)
    lower = jnp.concatenate([corner.T, lower_right], axis=1)
    return jnp.concatenate([upper, lower], axis=0)


def full_gram(block):
    high = lax.Precision.HIGHEST
    half = block.shape[1] // 2
    left = block[:, :half]
    right = block[:, half:]
    upper_left, corner, lower_right = lax.psum(
        (
            jnp.dot(left.T, left, precision=high),
            jnp.dot(left.T, right, precision=high),
            jnp.dot(right.T, right, precision=high),
        ),
        "rows",
    )
    return assemble(upper_left, corner, lower_right)


def local(snapshot, keep_side):
    high = lax.Precision.HIGHEST
    block = snapshot
    total_rows = block.shape[0] * lax.axis_size("rows")
    half = block.shape[1] // 2
    for turn in range(ROUNDS):
        gram = full_gram(block)
        rotation = polar_map(gram, total_rows)
        block = jnp.dot(block, rotation, precision=high)
        first = block[:, :half]
        second = block[:, half:]
        chosen = keep_side[turn, 0]
        forward = jnp.where(chosen == 0, first, second)
        backward = jnp.where(chosen == 0, second, first)
        arrived_fwd = shifted(forward, "pair", 1)
        arrived_bwd = shifted(backward, "pair", -1)
        block = jnp.concatenate([arrived_fwd, arrived_bwd], axis=1)
    return block


def solution(mesh):
    placed = (P("rows", "pair"), P(None, "pair"))
    return jax.shard_map(
        local, mesh=mesh, in_specs=placed, out_specs=P("rows", "pair"), check_vma=False
    )
```

profile of v0, /device:TPU:1, one launch (start us, length us, event | category | flops | bytes accessed | tf_op | source)
XLA Modules:
  0.0 278.3 jit_solution(8970609792271804935)
XLA Ops:
  6.5 2.4 fusion.44
  9.0 1.4 fusion.49
  10.4 1.4 fusion.46
  11.8 0.0 all-reduce.7.cloned.1.call-update
  11.8 0.0 all-reduce.5.cloned.1.call-start
  11.8 0.6 copy-done.6
  12.4 0.6 fusion.78
  13.6 90.0 %all-reduce.7.cloned.1.call-done = (f32[256,256]{1,0:T(8,128)}, f32[256,256]{0,1:T(8,128)}, f32[256,256]{1,0:T(8,128)}) async-done(((f32[256,256]{1,0:T(8,128)}, f32[256,256]{0,1:T(8,128)}, f32[256,256]{1,0:T(8,128)}), (f32[256,256]{1,0:T(8,128)}, f32[256,256]{0,1:T(8,128)}, f32[256,256]{1,0:T(8,128)})) %all-reduce.7.cloned.1.call-update) | async-done | bytes 786448 | tf_op jit(solution)/shard_map/psum | solution.py:49
  103.6 1.1 copy.9
  104.8 1.1 maximum_maximum_fusion
  105.9 0.0 copy-start.4
  105.9 4.7 %gather_fusion = f32[512]{0:T(512)S(1)} fusion(f32[512,512]{1,0:T(8,128)S(1)} %maximum_maximum_fusion, s32[512]{0:T(512)S(1)} %bitcast.26), kind=kCustom, calls=%fused_computation | custom fusion | bytes 8192 | tf_op jit(solution)/shard_map/jit(diagonal)/cond/branch_0_fun/gather | solution.py:21
  110.6 1.0 multiply_reduce_fusion.1
  112.4 2.2 fusion.74
  114.6 2.2 fusion.1
  116.7 2.1 fusion.5
  118.9 1.9 fusion.9
  120.8 1.9 fusion.2
  122.7 1.8 convolution_multiply_fusion.1
  124.6 1.2 convolution_bitcast_fusion
  125.8 7.9 %collective-permute-start.1 = (f32[192,256]{1,0:T(8,128)S(1)}, f32[192,256]{1,0:T(8,128)S(1)}, u32[]{:S(2)}, u32[]{:S(2)}) collective-permute-start(f32[192,256]{1,0:T(8,128)S(1)} %get-tuple-element.14), channel_id=1, source_target_pairs={{0,504},{8,0},{16,8},{24,16},{32,24},{40,32},{48,40},{56,48},{64,5... | collective-permute-start | bytes 589832 | tf_op jit(solution)/shard_map/ppermute | solution.py:15
  133.7 4.2 %collective-permute-start = (f32[192,256]{1,0:T(8,128)S(1)}, f32[192,256]{1,0:T(8,128)S(1)}, u32[]{:S(2)}, u32[]{:S(2)}) collective-permute-start(f32[192,256]{1,0:T(8,128)S(1)} %get-tuple-element.13), channel_id=1, source_target_pairs={{0,8},{8,16},{16,24},{24,32},{32,40},{40,48},{48,56},{56,64},{64,7... | collective-permute-start | bytes 589832 | tf_op jit(solution)/shard_map/ppermute | solution.py:15
  137.9 1.4 collective-permute-done.1
  139.3 1.4 fusion.81
  140.7 0.0 collective-permute-done
  140.7 1.4 fusion.80
  142.1 1.4 fusion.79
  143.5 0.0 all-reduce.5.cloned.1.call-update
  144.1 86.2 %all-reduce.5.cloned.1.call-done = (f32[256,256]{1,0:T(8,128)}, f32[256,256]{0,1:T(8,128)}, f32[256,256]{0,1:T(8,128)}) async-done(((f32[256,256]{1,0:T(8,128)}, f32[256,256]{0,1:T(8,128)}, f32[256,256]{0,1:T(8,128)}), (f32[256,256]{1,0:T(8,128)}, f32[256,256]{0,1:T(8,128)}, f32[256,256]{0,1:T(8,128)})) %all-reduce.5.cloned.1.call-update) | async-done | bytes 786448 | tf_op jit(solution)/shard_map/psum | solution.py:49
  230.4 1.1 pad_maximum_fusion
  231.5 0.2 copy.12
  231.7 0.7 copy-done.2
  232.4 0.1 copy-done.5
  232.5 0.1 maximum_maximum_fusion.1
  232.6 4.5 %gather_fusion.1 = f32[512]{0:T(512)S(1)} fusion(f32[512,512]{1,0:T(8,128)S(1)} %maximum_maximum_fusion.1, s32[512]{0:T(512)S(1)} %bitcast.27), kind=kCustom, calls=%fused_computation.1 | custom fusion | bytes 8192 | tf_op jit(solution)/shard_map/jit(diagonal)/cond/branch_0_fun/gather | solution.py:21
  237.1 1.0 multiply_reduce_fusion
  238.9 2.2 fusion.70
  241.0 2.2 fusion
  243.2 2.1 fusion.13
  245.4 1.9 fusion.17
  247.3 1.9 fusion.3
  249.2 1.9 convolution_multiply_fusion
  251.1 0.9 fusion.40
  252.0 10.2 %collective-permute-start.2 = (f32[192,256]{1,0:T(8,128)S(1)}, f32[192,256]{1,0:T(8,128)S(1)}, u32[]{:S(2)}, u32[]{:S(2)}) collective-permute-start(f32[192,256]{1,0:T(8,128)S(1)} %get-tuple-element.11), channel_id=1, source_target_pairs={{0,8},{8,16},{16,24},{24,32},{32,40},{40,48},{48,56},{56,64},{64,7... | collective-permute-start | bytes 589832 | tf_op jit(solution)/shard_map/ppermute | solution.py:15
  262.2 1.9 collective-permute-start.3
  264.1 0.7 collective-permute-done.2
  264.8 5.9 %collective-permute-done.3 = f32[192,256]{1,0:T(8,128)S(1)} collective-permute-done((f32[192,256]{1,0:T(8,128)S(1)}, f32[192,256]{1,0:T(8,128)S(1)}, u32[]{:S(2)}, u32[]{:S(2)}) %collective-permute-start.3) | collective-permute-done | bytes 196640 | tf_op jit(solution)/shard_map/ppermute | solution.py:15
  270.7 0.8 pad_maximum_fusion.1
  (18 shorter events, 0.1 us)
Async XLA Ops:
  6.5 2.4 copy-start
  6.5 97.1 %all-reduce.7.cloned.1.call-start = ((), (), s32[]{:S(2)}) async-start(), calls=%async_computation.1 | async-start | bytes 1572864 | tf_op jit(solution)/shard_map/psum | solution.py:49
  11.8 0.7 copy-start.6
  11.8 218.6 %all-reduce.5.cloned.1.call-start = ((), (), s32[]{:S(2)}) async-start(), calls=%async_computation | async-start | bytes 1572864 | tf_op jit(solution)/shard_map/psum | solution.py:49
  103.6 1.2 copy-start.1
  103.6 1.2 copy-start.3
  105.9 4.7 %copy-start.4 = (f32[256,256]{1,0:T(8,128)S(1)}, f32[256,256]{1,0:T(8,128)}, u32[]{:S(2)}) copy-start(f32[256,256]{1,0:T(8,128)} %get-tuple-element.10) | copy-start | bytes 786436
  125.8 13.5 %collective-permute-start.1 = (f32[192,256]{1,0:T(8,128)S(1)}, f32[192,256]{1,0:T(8,128)S(1)}, u32[]{:S(2)}, u32[]{:S(2)}) collective-permute-start(f32[192,256]{1,0:T(8,128)S(1)} %get-tuple-element.14), channel_id=1, source_target_pairs={{0,504},{8,0},{16,8},{24,16},{32,24},{40,32},{48,40},{56,48},{64,5... | collective-permute-start | bytes 589832 | tf_op jit(solution)/shard_map/ppermute | solution.py:15
  133.7 7.0 %collective-permute-start = (f32[192,256]{1,0:T(8,128)S(1)}, f32[192,256]{1,0:T(8,128)S(1)}, u32[]{:S(2)}, u32[]{:S(2)}) collective-permute-start(f32[192,256]{1,0:T(8,128)S(1)} %get-tuple-element.13), channel_id=1, source_target_pairs={{0,8},{8,16},{16,24},{24,32},{32,40},{40,48},{48,56},{56,64},{64,7... | collective-permute-start | bytes 589832 | tf_op jit(solution)/shard_map/ppermute | solution.py:15
  231.4 1.0 copy-start.2
  231.4 1.0 copy-start.5
  252.0 12.8 %collective-permute-start.2 = (f32[192,256]{1,0:T(8,128)S(1)}, f32[192,256]{1,0:T(8,128)S(1)}, u32[]{:S(2)}, u32[]{:S(2)}) collective-permute-start(f32[192,256]{1,0:T(8,128)S(1)} %get-tuple-element.11), channel_id=1, source_target_pairs={{0,8},{8,16},{16,24},{24,32},{32,40},{40,48},{48,56},{56,64},{64,7... | collective-permute-start | bytes 589832 | tf_op jit(solution)/shard_map/ppermute | solution.py:15
  262.2 8.5 %collective-permute-start.3 = (f32[192,256]{1,0:T(8,128)S(1)}, f32[192,256]{1,0:T(8,128)S(1)}, u32[]{:S(2)}, u32[]{:S(2)}) collective-permute-start(f32[192,256]{1,0:T(8,128)S(1)} %get-tuple-element.12), channel_id=1, source_target_pairs={{0,504},{8,0},{16,8},{24,16},{32,24},{40,32},{48,40},{56,48},{64,5... | collective-permute-start | bytes 589832 | tf_op jit(solution)/shard_map/ppermute | solution.py:15
Sparse Core Ops, SparseCore 0:
  11.9 91.6 all-reduce.6
  143.6 86.6 all-reduce.4
where the time goes:
time: 279 us; the launch traced here: 278 us
  waiting for transfers between devices  184 us (66%)
  matrix products  35.7 us (13%)
  starting transfers between devices  24.2 us (9%)
  between operations  16.4 us (6%)
  local copies, waits for them, and re-layouts  12.6 us (5%)
  other arithmetic  5.13 us (2%)
    psum x2, waiting for transfers between devices, full_gram(): lax.psum((jnp.dot(left.T, left, precision=high), jnp.dot(left.T, right, p...  176 us
    ppermute x4, starting transfers between devices, shifted(): return lax.ppermute(value, axis, pairs)  24.2 us
    gather x2, local copies, waits for them, and re-layouts, polar_map(): diag_vals = jnp.diagonal(gram)  9.23 us
    ppermute x4, waiting for transfers between devices, shifted(): return lax.ppermute(value, axis, pairs)  7.98 us
  transfers between devices with their start and end apart: 6, of which 5 were waited for; matrix products, arithmetic and copies ran while one was open for 1% of the time, Pallas kernels for 0%

commit v1 on v0

v1 whole, which is shorter than its diff:
```python
import jax
import jax.numpy as jnp
from jax import lax
from jax.experimental import pallas as pl
from jax.experimental.pallas import tpu as pltpu
from jax.sharding import PartitionSpec as P

ROUNDS = 2


EPS = 1e-06

ROW_PARTS = 8


def shifted(value, axis, steps):
    count = lax.axis_size(axis)
    pairs = [(source, (source + steps) % count) for source in range(count)]
    return lax.ppermute(value, axis, pairs)


def split(value):
    high = value.astype(jnp.bfloat16)
    return high, (value - high.astype(jnp.float32)).astype(jnp.bfloat16)


def dot(left, right):
    return jnp.dot(left, right, preferred_element_type=jnp.float32)


def dot3(left, right):
    left_high, left_low = left
    right_high, right_low = right
    small = dot(left_high, right_low) + dot(left_low, right_high)
    return dot(left_high, right_high) + small


def gram_kernel(left_ref, right_ref, out_ref):
    left = left_ref[...]
    right = right_ref[...]
    half = left.shape[1]
    mid = half // 2
    whole = split(jnp.concatenate([left, right], axis=1))
    left_t = split(left.T)
    right_t = split(right.T)
    upper = dot3(left_t, whole)
    lower = dot3(right_t, (whole[0][:, half:], whole[1][:, half:]))
    parts = out_ref.shape[0]
    rows = mid // parts
    spots = (
        upper[:mid, :half],
        upper[mid:, mid:half],
        lower[:mid],
        lower[mid:, mid:],
        upper[:mid, half:],
        upper[mid:, half:],
    )
    start = 0
    for spot in spots:
        width = spot.shape[1]
        out_ref[:, :, start : start + width] = spot.reshape(parts, rows, width)
        start += width


def sum_kernel(in_ref, out_ref):
    total = in_ref[0]
    for part in range(1, in_ref.shape[0]):
        total = total + in_ref[part]
    for part in range(out_ref.shape[0]):
        out_ref[part] = total


def unpack(packed):
    mid = packed.shape[0]
    a00, a01, a11, b00, b01, b11, c00, c01, c10, c11 = (
        packed[:, i * mid : (i + 1) * mid] for i in range(10)
    )
    rows = (
        (a00, a01, c00, c01),
        (a01.T, a11, c10, c11),
        (c00.T, c10.T, b00, b01),
        (c01.T, c11.T, b01.T, b11),
    )
    gram = jnp.concatenate([jnp.concatenate(row, axis=1) for row in rows], axis=0)
    return gram, (a00, a11, b00, b11)


def polar_kernel(total_rows, side_ref, packed_ref, left_ref, right_ref, fwd_ref, bwd_ref):
    parts, rows, width = packed_ref.shape
    gram, diag_blocks = unpack(packed_ref[...].reshape(parts * rows, width))
    size = gram.shape[0]
    mid = diag_blocks[0].shape[0]
    small_eye = lax.broadcasted_iota(jnp.int32, (mid, mid), 0) == lax.broadcasted_iota(
        jnp.int32, (mid, mid), 1
    )
    picked = [jnp.where(small_eye, block, 0.0) for block in diag_blocks]
    along = jnp.concatenate([jnp.sum(p, axis=0, keepdims=True) for p in picked], axis=1)
    down = jnp.concatenate([jnp.sum(p, axis=1, keepdims=True) for p in picked], axis=0)
    inv_along = lax.rsqrt(along / total_rows + EPS)
    inv_down = lax.rsqrt(down / total_rows + EPS)
    corr = gram * inv_down * inv_along * (1.0 / total_rows)
    square = jnp.sum(jnp.sum(corr * corr, axis=0, keepdims=True), axis=1, keepdims=True)
    scale = jnp.sqrt(square / size)
    eye = lax.broadcasted_iota(jnp.int32, (size, size), 0) == lax.broadcasted_iota(
        jnp.int32, (size, size), 1
    )
    dev = corr * (1.0 / scale) - jnp.where(eye, 1.0, 0.0)
    dev_s = split(dev)
    dev_two = dot3(dev_s, dev_s)
    factor = 0.0625 * dev_two - 0.3125 * dev + jnp.where(eye, 0.375, 0.0)
    z_dev = dot3(split(dev_two), split(factor)) - 0.5 * dev
    z_s = split(z_dev)
    block = jnp.concatenate([left_ref[...], right_ref[...]], axis=1)
    block = block * (inv_along * lax.rsqrt(scale))
    first = block + dot3(split(block), z_s)
    turned = first + dot3(split(first), dev_s)
    turned = turned + dot3(split(turned), z_s)
    turned = turned + dot3(split(turned), z_s)
    new = 1.5 * first - 0.5 * turned
    half = size // 2
    kept = side_ref[0] == 0
    fwd_ref[...] = jnp.where(kept, new[:, :half], new[:, half:])
    bwd_ref[...] = jnp.where(kept, new[:, half:], new[:, :half])


def vmem(count):
    return [pl.BlockSpec(memory_space=pltpu.VMEM)] * count


def local(snapshot, keep_side):
    parts = lax.axis_size("rows")
    rows, size = snapshot.shape
    total_rows = rows * parts
    half = size // 2
    mid = half // 2
    left, right = snapshot[:, :half], snapshot[:, half:]
    packed_shape = jax.ShapeDtypeStruct((parts, mid // parts, 10 * mid), jnp.float32)
    half_shape = jax.ShapeDtypeStruct((rows, half), jnp.float32)
    for turn in range(ROUNDS):
        partial = pl.pallas_call(
            gram_kernel,
            out_shape=packed_shape,
            in_specs=vmem(2),
            out_specs=vmem(1)[0],
            name="gram",
        )(left, right)
        terms = lax.all_to_all(partial, "rows", 0, 0)
        summed = pl.pallas_call(
            sum_kernel,
            out_shape=packed_shape,
            in_specs=vmem(1),
            out_specs=vmem(1)[0],
            name="sum",
        )(terms)
        gathered = lax.all_to_all(summed, "rows", 0, 0)
        forward, backward = pl.pallas_call(
            lambda *refs: polar_kernel(float(total_rows), *refs),
            out_shape=(half_shape, half_shape),
            in_specs=[pl.BlockSpec(memory_space=pltpu.SMEM)] + vmem(3),
            out_specs=tuple(vmem(2)),
            name="polar",
        )(keep_side[turn], gathered, left, right)
        left = shifted(forward, "pair", 1)
        right = shifted(backward, "pair", -1)
    return jnp.concatenate([left, right], axis=1)


def solution(mesh):
    placed = (P("rows", "pair"), P(None, "pair"))
    return jax.shard_map(
        local, mesh=mesh, in_specs=placed, out_specs=P("rows", "pair"), check_vma=False
    )
```

time: 279 us -> 119 us (0.43)
  waiting for transfers between devices: 184 us -> 22.7 us
  blocking collectives: 0 us -> 40 us
  matrix products: 35.7 us -> 0 us
  Pallas kernels: 0 us -> 22.5 us
  between operations: 16.4 us -> 0.06 us
  local copies, waits for them, and re-layouts: 12.6 us -> 3.96 us
  other arithmetic: 5.13 us -> 0.79 us
    psum x2 -> x0, waiting for transfers between devices: 176 us -> none  [full_gram(): lax.psum((jnp.dot(left.T, left, precision=high), jnp.dot(left.T, right, p...]
    all_to_all x0 -> x3, blocking collectives: none -> 40 us  [the longest x2 27.6 us: local(): terms = lax.all_to_all(partial, 'rows', 0, 0)]
    dot_general x20 -> x0, matrix products: 35.7 us -> none  [the longest x2 4.37 us: polar_map(): e_two = jnp.dot(e_mat, e_mat, precision=high)]
    pallas_call x0 -> x6, Pallas kernels: none -> 22.5 us  [the longest x2 13.7 us: local(): pl.pallas_call(lambda *refs: polar_kernel(float(total_rows), *refs), out_...]
    gather x2 -> x0, local copies, waits for them, and re-layouts: 9.23 us -> none  [polar_map(): diag_vals = jnp.diagonal(gram)]
    ppermute x4, waiting for transfers between devices: 7.98 us -> 15.7 us  [shifted(): return lax.ppermute(value, axis, pairs)]
    all_to_all x0 -> x1, waiting for transfers between devices: none -> 7.02 us  [local(): gathered = lax.all_to_all(summed, 'rows', 0, 0)]
    all_to_all x0 -> x1, starting transfers between devices: none -> 3.67 us  [local(): gathered = lax.all_to_all(summed, 'rows', 0, 0)]
  transfers between devices with their start and end apart: 6 -> 5, of which waited for: 5 -> 5; matrix products, arithmetic and copies ran while one was open for 1% -> 1% of each run, Pallas kernels for 0% -> 0%
where the time goes in v1:
time: 119 us; the launch traced here: 117 us
  blocking collectives  40 us (34%)
  starting transfers between devices  26.7 us (22%)
  waiting for transfers between devices  22.7 us (19%)
  Pallas kernels  22.5 us (19%)
  local copies, waits for them, and re-layouts  3.96 us (3%)
    all_to_all x2, blocking collectives, local(): terms = lax.all_to_all(partial, 'rows', 0, 0)  27.6 us
    ppermute x4, starting transfers between devices, shifted(): return lax.ppermute(value, axis, pairs)  23 us
    ppermute x4, waiting for transfers between devices, shifted(): return lax.ppermute(value, axis, pairs)  15.7 us
    pallas_call x2, Pallas kernels, local(): pl.pallas_call(lambda *refs: polar_kernel(float(total_rows), *refs), out_...  13.7 us
    all_to_all x1, blocking collectives, local(): gathered = lax.all_to_all(summed, 'rows', 0, 0)  12.5 us
    all_to_all x1, waiting for transfers between devices, local(): gathered = lax.all_to_all(summed, 'rows', 0, 0)  7.02 us
    pallas_call x2, Pallas kernels, local(): pl.pallas_call(gram_kernel, out_shape=packed_shape, in_specs=vmem(2), out...  4.8 us
    pallas_call x2, Pallas kernels, local(): pl.pallas_call(sum_kernel, out_shape=packed_shape, in_specs=vmem(1), out_...  3.98 us
  transfers between devices with their start and end apart: 5, of which 5 were waited for; matrix products, arithmetic and copies ran while one was open for 1% of the time, Pallas kernels for 0%

profile of v1, /device:TPU:1, one launch (start us, length us, event | category | flops | bytes accessed | tf_op | source)
XLA Modules:
  0.0 116.7 jit_solution(8412234217109460991)
XLA Ops:
  0.0 1.8 %fusion = (f32[192,256]{1,0:T(8,128)}, f32[192,256]{1,0:T(8,128)}) fusion(f32[192,512]{1,0:T(8,128)} %param.2), kind=kLoop, calls=%fused_computation.1 | loop fusion | bytes 786432 | tf_op jit(solution)/shard_map/slice | solution.py:136
  1.8 2.4 %gram.2 = f32[8,16,1280]{2,1,0:T(8,128)} custom-call(f32[192,256]{1,0:T(8,128)} %get-tuple-element.14.left_ref.refs_2_, f32[192,256]{1,0:T(8,128)} %get-tuple-element.13.right_ref.refs_3_), custom_call_target="tpu_custom_call" | custom-call | tf_op jit(solution)/shard_map/gram/pallas_call | solution.py:140
  4.2 14.0 %all_to_all.20.in_ref = f32[8,16,1280]{2,1,0:T(8,128)} all-to-all(f32[8,16,1280]{2,1,0:T(8,128)} %gram.2), channel_id=1, replica_groups=mesh['pair'=64,'rows'=8] {'rows'}, dimensions={0} | all-to-all | bytes 1310720 | tf_op jit(solution)/shard_map/all_to_all | solution.py:147
  18.2 2.0 %sum.2 = f32[8,16,1280]{2,1,0:T(8,128)} custom-call(f32[8,16,1280]{2,1,0:T(8,128)} %all_to_all.20.in_ref), custom_call_target="tpu_custom_call" | custom-call | tf_op jit(solution)/shard_map/sum/pallas_call | solution.py:148
  20.2 0.0 copy-start.3
  20.2 3.7 %all-to-all-start.1 = ((f32[8,16,1280]{2,1,0:T(8,128)}), f32[8,16,1280]{2,1,0:T(8,128)S(1)}, u32[]{:S(2)}, u32[]{:S(2)}) async-start(f32[8,16,1280]{2,1,0:T(8,128)} %sum.2), calls=%async_computation.1 | async-start | bytes 1310720 | tf_op jit(solution)/shard_map/all_to_all | solution.py:155
  23.9 0.0 copy-done.3
  23.9 0.6 fusion.1
  24.5 7.0 %all-to-all-done.1.refs_1_ = f32[8,16,1280]{2,1,0:T(8,128)S(1)} async-done(((f32[8,16,1280]{2,1,0:T(8,128)}), f32[8,16,1280]{2,1,0:T(8,128)S(1)}, u32[]{:S(2)}, u32[]{:S(2)}) %all-to-all-start.1) | async-done | bytes 655392 | tf_op jit(solution)/shard_map/all_to_all | solution.py:155
  31.5 0.0 copy-start
  31.5 0.8 copy-done
  32.4 6.8 %polar.2 = (f32[192,256]{1,0:T(8,128)}, f32[192,256]{1,0:T(8,128)}) custom-call(s32[1]{0:T(128)} %bitcast.1.refs_0_, f32[8,16,1280]{2,1,0:T(8,128)} %copy-done, f32[192,256]{1,0:T(8,128)} %get-tuple-element.14.left_ref.refs_2_, f32[192,256]{1,0:T(8,128)} %get-tuple-element.13.right_ref.refs_3_), custom_call_target="tpu_custom_call" | custom-call | tf_op jit(solution)/shard_map/polar/pallas_call | solution.py:156
  39.2 10.6 %collective-permute-start = (f32[192,256]{1,0:T(8,128)}, f32[192,256]{1,0:T(8,128)S(1)}, u32[]{:S(2)}, u32[]{:S(2)}) collective-permute-start(f32[192,256]{1,0:T(8,128)} %get-tuple-element.9), channel_id=1, source_target_pairs={{0,8},{8,16},{16,24},{24,32},{32,40},{40,48},{48,56},{56,64},{64,7... | collective-permute-start | bytes 589832 | tf_op jit(solution)/shard_map/ppermute | solution.py:19
  49.8 1.9 %collective-permute-start.1 = (f32[192,256]{1,0:T(8,128)}, f32[192,256]{1,0:T(8,128)S(1)}, u32[]{:S(2)}, u32[]{:S(2)}) collective-permute-start(f32[192,256]{1,0:T(8,128)} %get-tuple-element.10), channel_id=1, source_target_pairs={{0,504},{8,0},{16,8},{24,16},{32,24},{40,32},{48,40},{56,48},{64,5... | collective-permute-start | bytes 589832 | tf_op jit(solution)/shard_map/ppermute | solution.py:19
  51.7 1.0 collective-permute-done.left_ref.refs_2_
  52.7 0.0 copy-start.1
  52.7 7.9 %collective-permute-done.1.right_ref.refs_3_ = f32[192,256]{1,0:T(8,128)S(1)} collective-permute-done((f32[192,256]{1,0:T(8,128)}, f32[192,256]{1,0:T(8,128)S(1)}, u32[]{:S(2)}, u32[]{:S(2)}) %collective-permute-start.1) | collective-permute-done | bytes 196640 | tf_op jit(solution)/shard_map/ppermute | solution.py:19
  60.6 0.0 copy-done.1
  60.6 0.0 copy-start.2
  60.6 0.7 copy-done.2
  61.3 2.4 %gram.3 = f32[8,16,1280]{2,1,0:T(8,128)} custom-call(f32[192,256]{1,0:T(8,128)} %copy-done.1, f32[192,256]{1,0:T(8,128)} %copy-done.2), custom_call_target="tpu_custom_call" | custom-call | tf_op jit(solution)/shard_map/gram/pallas_call | solution.py:140
  63.7 13.5 %all_to_all.21.in_ref = f32[8,16,1280]{2,1,0:T(8,128)} all-to-all(f32[8,16,1280]{2,1,0:T(8,128)} %gram.3), channel_id=1, replica_groups=mesh['pair'=64,'rows'=8] {'rows'}, dimensions={0} | all-to-all | bytes 1310720 | tf_op jit(solution)/shard_map/all_to_all | solution.py:147
  77.2 2.0 %sum.3 = f32[8,16,1280]{2,1,0:T(8,128)} custom-call(f32[8,16,1280]{2,1,0:T(8,128)} %all_to_all.21.in_ref), custom_call_target="tpu_custom_call" | custom-call | tf_op jit(solution)/shard_map/sum/pallas_call | solution.py:148
  79.2 12.5 %all_to_all.22.refs_1_ = f32[8,16,1280]{2,1,0:T(8,128)} all-to-all(f32[8,16,1280]{2,1,0:T(8,128)} %sum.3), channel_id=1, replica_groups=mesh['pair'=64,'rows'=8] {'rows'}, dimensions={0} | all-to-all | bytes 1310720 | tf_op jit(solution)/shard_map/all_to_all | solution.py:155
  91.7 6.9 %polar.3 = (f32[192,256]{1,0:T(8,128)}, f32[192,256]{1,0:T(8,128)}) custom-call(s32[1]{0:T(128)} %bitcast.refs_0_, f32[8,16,1280]{2,1,0:T(8,128)} %all_to_all.22.refs_1_, f32[192,256]{1,0:T(8,128)} %copy-done.1, f32[192,256]{1,0:T(8,128)} %copy-done.2), custom_call_target="tpu_custom_call" | custom-call | tf_op jit(solution)/shard_map/polar/pallas_call | solution.py:156
  98.6 8.6 %collective-permute-start.2 = (f32[192,256]{1,0:T(8,128)}, f32[192,256]{1,0:T(8,128)S(1)}, u32[]{:S(2)}, u32[]{:S(2)}) collective-permute-start(f32[192,256]{1,0:T(8,128)} %get-tuple-element.11), channel_id=1, source_target_pairs={{0,8},{8,16},{16,24},{24,32},{32,40},{40,48},{48,56},{56,64},{64,7... | collective-permute-start | bytes 589832 | tf_op jit(solution)/shard_map/ppermute | solution.py:19
  107.2 1.9 %collective-permute-start.3 = (f32[192,256]{1,0:T(8,128)}, f32[192,256]{1,0:T(8,128)S(1)}, u32[]{:S(2)}, u32[]{:S(2)}) collective-permute-start(f32[192,256]{1,0:T(8,128)} %get-tuple-element.12), channel_id=1, source_target_pairs={{0,504},{8,0},{16,8},{24,16},{32,24},{40,32},{48,40},{56,48},{64,5... | collective-permute-start | bytes 589832 | tf_op jit(solution)/shard_map/ppermute | solution.py:19
  109.1 1.0 collective-permute-done.2
  110.1 5.8 %collective-permute-done.3 = f32[192,256]{1,0:T(8,128)S(1)} collective-permute-done((f32[192,256]{1,0:T(8,128)}, f32[192,256]{1,0:T(8,128)S(1)}, u32[]{:S(2)}, u32[]{:S(2)}) %collective-permute-start.3) | collective-permute-done | bytes 196640 | tf_op jit(solution)/shard_map/ppermute | solution.py:19
  115.9 0.8 pad_maximum_fusion
Async XLA Ops:
  20.2 3.7 %copy-start.3 = (s32[2,1]{0,1:T(1,128)S(1)}, s32[2,1]{0,1:T(1,128)}, u32[]{:S(2)}) copy-start(s32[2,1]{0,1:T(1,128)} %param.3) | copy-start | bytes 28
  20.2 11.4 %all-to-all-start.1 = ((f32[8,16,1280]{2,1,0:T(8,128)}), f32[8,16,1280]{2,1,0:T(8,128)S(1)}, u32[]{:S(2)}, u32[]{:S(2)}) async-start(f32[8,16,1280]{2,1,0:T(8,128)} %sum.2), calls=%async_computation.1 | async-start | bytes 1310720 | tf_op jit(solution)/shard_map/all_to_all | solution.py:155
  31.5 0.9 copy-start
  39.2 13.5 %collective-permute-start = (f32[192,256]{1,0:T(8,128)}, f32[192,256]{1,0:T(8,128)S(1)}, u32[]{:S(2)}, u32[]{:S(2)}) collective-permute-start(f32[192,256]{1,0:T(8,128)} %get-tuple-element.9), channel_id=1, source_target_pairs={{0,8},{8,16},{16,24},{24,32},{32,40},{40,48},{48,56},{56,64},{64,7... | collective-permute-start | bytes 589832 | tf_op jit(solution)/shard_map/ppermute | solution.py:19
  49.8 10.8 %collective-permute-start.1 = (f32[192,256]{1,0:T(8,128)}, f32[192,256]{1,0:T(8,128)S(1)}, u32[]{:S(2)}, u32[]{:S(2)}) collective-permute-start(f32[192,256]{1,0:T(8,128)} %get-tuple-element.10), channel_id=1, source_target_pairs={{0,504},{8,0},{16,8},{24,16},{32,24},{40,32},{48,40},{56,48},{64,5... | collective-permute-start | bytes 589832 | tf_op jit(solution)/shard_map/ppermute | solution.py:19
  52.7 7.9 %copy-start.1 = (f32[192,256]{1,0:T(8,128)}, f32[192,256]{1,0:T(8,128)S(1)}, u32[]{:S(2)}) copy-start(f32[192,256]{1,0:T(8,128)S(1)} %collective-permute-done.left_ref.refs_2_) | copy-start | bytes 589828
  60.6 0.7 copy-start.2
  98.6 11.5 %collective-permute-start.2 = (f32[192,256]{1,0:T(8,128)}, f32[192,256]{1,0:T(8,128)S(1)}, u32[]{:S(2)}, u32[]{:S(2)}) collective-permute-start(f32[192,256]{1,0:T(8,128)} %get-tuple-element.11), channel_id=1, source_target_pairs={{0,8},{8,16},{16,24},{24,32},{32,40},{40,48},{48,56},{56,64},{64,7... | collective-permute-start | bytes 589832 | tf_op jit(solution)/shard_map/ppermute | solution.py:19
  107.2 8.7 %collective-permute-start.3 = (f32[192,256]{1,0:T(8,128)}, f32[192,256]{1,0:T(8,128)S(1)}, u32[]{:S(2)}, u32[]{:S(2)}) collective-permute-start(f32[192,256]{1,0:T(8,128)} %get-tuple-element.12), channel_id=1, source_target_pairs={{0,504},{8,0},{16,8},{24,16},{32,24},{40,32},{48,40},{56,48},{64,5... | collective-permute-start | bytes 589832 | tf_op jit(solution)/shard_map/ppermute | solution.py:19

commit v2 on v1

--- a/solution.py
+++ b/solution.py
@@ -1,3 +1,5 @@
+import functools
+
 import jax
 import jax.numpy as jnp
 from jax import lax
@@ -35,14 +37,18 @@
     return dot(left_high, right_high) + small
 
 
-def gram_kernel(left_ref, right_ref, out_ref):
-    left = left_ref[...]
-    right = right_ref[...]
-    half = left.shape[1]
+def joined(refs):
+    return jnp.concatenate([ref[...] for ref in refs], axis=1)
+
+
+def gram_kernel(*refs):
+    *block_refs, out_ref = refs
+    block = joined(block_refs)
+    half = block.shape[1] // 2
     mid = half // 2
-    whole = split(jnp.concatenate([left, right], axis=1))
-    left_t = split(left.T)
-    right_t = split(right.T)
+    whole = split(block)
+    left_t = split(block[:, :half].T)
+    right_t = split(block[:, half:].T)
     upper = dot3(left_t, whole)
     lower = dot3(right_t, (whole[0][:, half:], whole[1][:, half:]))
     parts = out_ref.shape[0]
@@ -85,7 +91,8 @@
     return gram, (a00, a11, b00, b11)
 
 
-def polar_kernel(total_rows, side_ref, packed_ref, left_ref, right_ref, fwd_ref, bwd_ref):
+def polar_kernel(total_rows, turn, side_ref, packed_ref, *refs):
+    *block_refs, fwd_ref, bwd_ref = refs
     parts, rows, width = packed_ref.shape
     gram, diag_blocks = unpack(packed_ref[...].reshape(parts * rows, width))
     size = gram.shape[0]
@@ -110,15 +117,14 @@
     factor = 0.0625 * dev_two - 0.3125 * dev + jnp.where(eye, 0.375, 0.0)
     z_dev = dot3(split(dev_two), split(factor)) - 0.5 * dev
     z_s = split(z_dev)
-    block = jnp.concatenate([left_ref[...], right_ref[...]], axis=1)
-    block = block * (inv_along * lax.rsqrt(scale))
+    block = joined(block_refs) * (inv_along * lax.rsqrt(scale))
     first = block + dot3(split(block), z_s)
     turned = first + dot3(split(first), dev_s)
     turned = turned + dot3(split(turned), z_s)
     turned = turned + dot3(split(turned), z_s)
     new = 1.5 * first - 0.5 * turned
     half = size // 2
-    kept = side_ref[0] == 0
+    kept = side_ref[turn] == 0
     fwd_ref[...] = jnp.where(kept, new[:, :half], new[:, half:])
     bwd_ref[...] = jnp.where(kept, new[:, half:], new[:, :half])
 
@@ -127,23 +133,29 @@
     return [pl.BlockSpec(memory_space=pltpu.VMEM)] * count
 
 
+def room(mib):
+    return pltpu.CompilerParams(vmem_limit_bytes=mib * 2**20)
+
+
 def local(snapshot, keep_side):
     parts = lax.axis_size("rows")
     rows, size = snapshot.shape
     total_rows = rows * parts
     half = size // 2
     mid = half // 2
-    left, right = snapshot[:, :half], snapshot[:, half:]
+    blocks = (snapshot,)
+    sides = keep_side.reshape(keep_side.shape[0])
     packed_shape = jax.ShapeDtypeStruct((parts, mid // parts, 10 * mid), jnp.float32)
     half_shape = jax.ShapeDtypeStruct((rows, half), jnp.float32)
     for turn in range(ROUNDS):
         partial = pl.pallas_call(
             gram_kernel,
             out_shape=packed_shape,
-            in_specs=vmem(2),
+            in_specs=vmem(len(blocks)),
             out_specs=vmem(1)[0],
             name="gram",
-        )(left, right)
+            compiler_params=room(8),
+        )(*blocks)
         terms = lax.all_to_all(partial, "rows", 0, 0)
         summed = pl.pallas_call(
             sum_kernel,
@@ -151,18 +163,19 @@
             in_specs=vmem(1),
             out_specs=vmem(1)[0],
             name="sum",
+            compiler_params=room(8),
         )(terms)
         gathered = lax.all_to_all(summed, "rows", 0, 0)
         forward, backward = pl.pallas_call(
-            lambda *refs: polar_kernel(float(total_rows), *refs),
+            functools.partial(polar_kernel, float(total_rows), turn),
             out_shape=(half_shape, half_shape),
-            in_specs=[pl.BlockSpec(memory_space=pltpu.SMEM)] + vmem(3),
+            in_specs=[pl.BlockSpec(memory_space=pltpu.SMEM)] + vmem(1 + len(blocks)),
             out_specs=tuple(vmem(2)),
             name="polar",
-        )(keep_side[turn], gathered, left, right)
-        left = shifted(forward, "pair", 1)
-        right = shifted(backward, "pair", -1)
-    return jnp.concatenate([left, right], axis=1)
+            compiler_params=room(24),
+        )(sides, gathered, *blocks)
+        blocks = (shifted(forward, "pair", 1), shifted(backward, "pair", -1))
+    return jnp.concatenate(blocks, axis=1)
 
 
 def solution(mesh):

time: 119 us -> 101 us (0.85)
  Pallas kernels: 22.5 us -> 10.7 us
  blocking collectives: 40 us -> 48.4 us
  waiting for transfers between devices: 22.7 us -> 15.2 us
  starting transfers between devices: 26.7 us -> 22 us
  local copies, waits for them, and re-layouts: 3.96 us -> 1.65 us
    all_to_all x1 -> x2, blocking collectives: 12.5 us -> 22.3 us  [local(): gathered = lax.all_to_all(summed, 'rows', 0, 0)]
    pallas_call x4, Pallas kernels: 18.5 us -> 10.6 us  [the longest x2 9.6 us: local(): pl.pallas_call(functools.partial(polar_kernel, float(total_rows), turn),...]
    all_to_all x1 -> x0, waiting for transfers between devices: 7.02 us -> none  [local(): gathered = lax.all_to_all(summed, 'rows', 0, 0)]
    pallas_call x2, Pallas kernels: 3.98 us -> 0.1 us  [local(): pl.pallas_call(sum_kernel, out_shape=packed_shape, in_specs=vmem(1), out_...]
    all_to_all x1 -> x0, starting transfers between devices: 3.67 us -> none  [local(): gathered = lax.all_to_all(summed, 'rows', 0, 0)]
    slice x2 -> x0, local copies, waits for them, and re-layouts: 2.43 us -> none  [the longest x1 1.78 us: local(): left, right = (snapshot[:, :half], snapshot[:, half:])]
    all_to_all x2, blocking collectives: 27.6 us -> 26.2 us  [local(): terms = lax.all_to_all(partial, 'rows', 0, 0)]
  transfers between devices with their start and end apart: 5 -> 4, of which waited for: 5 -> 4; matrix products, arithmetic and copies ran while one was open for 1% -> 0% of each run, Pallas kernels for 0% -> 0%
where the time goes in v2:
time: 101 us; the launch traced here: 98.9 us
  blocking collectives  48.4 us (48%)
  starting transfers between devices  22 us (22%)
  waiting for transfers between devices  15.2 us (15%)
  Pallas kernels  10.7 us (11%)
  local copies, waits for them, and re-layouts  1.65 us (2%)
    all_to_all x2, blocking collectives, local(): terms = lax.all_to_all(partial, 'rows', 0, 0)  26.2 us
    all_to_all x2, blocking collectives, local(): gathered = lax.all_to_all(summed, 'rows', 0, 0)  22.3 us
    ppermute x4, starting transfers between devices, shifted(): return lax.ppermute(value, axis, pairs)  22 us
    ppermute x4, waiting for transfers between devices, shifted(): return lax.ppermute(value, axis, pairs)  15.2 us
    pallas_call x2, Pallas kernels, local(): pl.pallas_call(functools.partial(polar_kernel, float(total_rows), turn),...  9.6 us
  transfers between devices with their start and end apart: 4, of which 4 were waited for; matrix products, arithmetic and copies ran while one was open for 0% of the time, Pallas kernels for 0%

profile of v2, /device:TPU:1, one launch (start us, length us, event | category | flops | bytes accessed | tf_op | source)
XLA Modules:
  0.0 98.9 jit_solution(16937921292601204666)
XLA Ops:
  0.0 0.0 copy-start
  0.0 1.0 %copy-done = f32[192,512]{1,0:T(8,128)S(1)} copy-done((f32[192,512]{1,0:T(8,128)S(1)}, f32[192,512]{1,0:T(8,128)}, u32[]{:S(2)}) %copy-start) | copy-done | bytes 393240
  1.0 0.5 gram.2
  1.5 13.7 %all_to_all.20.in_ref = f32[8,16,1280]{2,1,0:T(8,128)S(1)} all-to-all(f32[8,16,1280]{2,1,0:T(8,128)S(1)} %gram.2), channel_id=1, replica_groups=mesh['pair'=64,'rows'=8] {'rows'}, dimensions={0} | all-to-all | bytes 1310720 | tf_op jit(solution)/shard_map/all_to_all | solution.py:159
  15.2 0.1 sum.2
  15.3 0.0 copy-start.1
  15.3 10.8 %all_to_all.21.packed_ref = f32[8,16,1280]{2,1,0:T(8,128)S(1)} all-to-all(f32[8,16,1280]{2,1,0:T(8,128)S(1)} %sum.2), channel_id=1, replica_groups=mesh['pair'=64,'rows'=8] {'rows'}, dimensions={0} | all-to-all | bytes 1310720 | tf_op jit(solution)/shard_map/all_to_all | solution.py:168
  26.1 0.0 copy-start.2
  26.1 0.0 copy-done.1
  26.1 0.7 copy-done.2
  26.7 4.8 %polar.2 = (f32[192,256]{1,0:T(8,128)S(1)}, f32[192,256]{1,0:T(8,128)S(1)}) custom-call(s32[2]{0:T(128)S(1)} %bitcast.1, f32[8,16,1280]{2,1,0:T(8,128)S(1)} %all_to_all.21.packed_ref, f32[192,512]{1,0:T(8,128)S(1)} %copy-done.1), custom_call_target="tpu_custom_call" | custom-call | tf_op jit(solution)/shard_map/polar/pallas_call | solution.py:169
  31.5 10.9 %collective-permute-start = (f32[192,256]{1,0:T(8,128)S(1)}, f32[192,256]{1,0:T(8,128)S(1)}, u32[]{:S(2)}, u32[]{:S(2)}) collective-permute-start(f32[192,256]{1,0:T(8,128)S(1)} %get-tuple-element.9), channel_id=1, source_target_pairs={{0,8},{8,16},{16,24},{24,32},{32,40},{40,48},{48,56},{56,64},{64,7... | collective-permute-start | bytes 589832 | tf_op jit(solution)/shard_map/ppermute | solution.py:21
  42.5 1.9 %collective-permute-start.1 = (f32[192,256]{1,0:T(8,128)S(1)}, f32[192,256]{1,0:T(8,128)S(1)}, u32[]{:S(2)}, u32[]{:S(2)}) collective-permute-start(f32[192,256]{1,0:T(8,128)S(1)} %get-tuple-element.10), channel_id=1, source_target_pairs={{0,504},{8,0},{16,8},{24,16},{32,24},{40,32},{48,40},{56,48},{64,5... | collective-permute-start | bytes 589832 | tf_op jit(solution)/shard_map/ppermute | solution.py:21
  44.4 0.7 collective-permute-done.refs_0_
  45.0 8.0 %collective-permute-done.1.refs_1_ = f32[192,256]{1,0:T(8,128)S(1)} collective-permute-done((f32[192,256]{1,0:T(8,128)S(1)}, f32[192,256]{1,0:T(8,128)S(1)}, u32[]{:S(2)}, u32[]{:S(2)}) %collective-permute-start.1) | collective-permute-done | bytes 196640 | tf_op jit(solution)/shard_map/ppermute | solution.py:21
  53.1 0.5 gram.3
  53.6 12.5 %all_to_all.22.in_ref = f32[8,16,1280]{2,1,0:T(8,128)S(1)} all-to-all(f32[8,16,1280]{2,1,0:T(8,128)S(1)} %gram.3), channel_id=1, replica_groups=mesh['pair'=64,'rows'=8] {'rows'}, dimensions={0} | all-to-all | bytes 1310720 | tf_op jit(solution)/shard_map/all_to_all | solution.py:159
  66.0 0.1 sum.3
  66.1 11.5 %all_to_all.23.packed_ref = f32[8,16,1280]{2,1,0:T(8,128)S(1)} all-to-all(f32[8,16,1280]{2,1,0:T(8,128)S(1)} %sum.3), channel_id=1, replica_groups=mesh['pair'=64,'rows'=8] {'rows'}, dimensions={0} | all-to-all | bytes 1310720 | tf_op jit(solution)/shard_map/all_to_all | solution.py:168
  77.6 4.8 %polar.3 = (f32[192,256]{1,0:T(8,128)S(1)}, f32[192,256]{1,0:T(8,128)S(1)}) custom-call(s32[2]{0:T(128)S(1)} %bitcast.2, f32[8,16,1280]{2,1,0:T(8,128)S(1)} %all_to_all.23.packed_ref, f32[192,256]{1,0:T(8,128)S(1)} %collective-permute-done.refs_0_, f32[192,256]{1,0:T(8,128)S(1)} %collective-permute-done.1.refs_1_), custom_call_target="tpu_custom_call" | custom-call | tf_op jit(solution)/shard_map/polar/pallas_call | solution.py:169
  82.4 7.2 %collective-permute-start.2 = (f32[192,256]{1,0:T(8,128)S(1)}, f32[192,256]{1,0:T(8,128)S(1)}, u32[]{:S(2)}, u32[]{:S(2)}) collective-permute-start(f32[192,256]{1,0:T(8,128)S(1)} %get-tuple-element.11), channel_id=1, source_target_pairs={{0,8},{8,16},{16,24},{24,32},{32,40},{40,48},{48,56},{56,64},{64,7... | collective-permute-start | bytes 589832 | tf_op jit(solution)/shard_map/ppermute | solution.py:21
  89.7 1.9 %collective-permute-start.3 = (f32[192,256]{1,0:T(8,128)S(1)}, f32[192,256]{1,0:T(8,128)S(1)}, u32[]{:S(2)}, u32[]{:S(2)}) collective-permute-start(f32[192,256]{1,0:T(8,128)S(1)} %get-tuple-element.12), channel_id=1, source_target_pairs={{0,504},{8,0},{16,8},{24,16},{32,24},{40,32},{48,40},{56,48},{64,5... | collective-permute-start | bytes 589832 | tf_op jit(solution)/shard_map/ppermute | solution.py:21
  91.6 0.7 collective-permute-done.2
  92.2 5.9 %collective-permute-done.3 = f32[192,256]{1,0:T(8,128)S(1)} collective-permute-done((f32[192,256]{1,0:T(8,128)S(1)}, f32[192,256]{1,0:T(8,128)S(1)}, u32[]{:S(2)}, u32[]{:S(2)}) %collective-permute-start.3) | collective-permute-done | bytes 196640 | tf_op jit(solution)/shard_map/ppermute | solution.py:21
  98.1 0.8 pad_maximum_fusion
Async XLA Ops:
  0.0 1.0 %copy-start = (f32[192,512]{1,0:T(8,128)S(1)}, f32[192,512]{1,0:T(8,128)}, u32[]{:S(2)}) copy-start(f32[192,512]{1,0:T(8,128)} %refs_0_.3) | copy-start | bytes 1179652
  15.3 10.8 %copy-start.1 = (f32[192,512]{1,0:T(8,128)S(1)}, f32[192,512]{1,0:T(8,128)}, u32[]{:S(2)}) copy-start(f32[192,512]{1,0:T(8,128)} %refs_0_.3) | copy-start | bytes 1179652
  26.1 0.7 copy-start.2
  31.5 13.5 %collective-permute-start = (f32[192,256]{1,0:T(8,128)S(1)}, f32[192,256]{1,0:T(8,128)S(1)}, u32[]{:S(2)}, u32[]{:S(2)}) collective-permute-start(f32[192,256]{1,0:T(8,128)S(1)} %get-tuple-element.9), channel_id=1, source_target_pairs={{0,8},{8,16},{16,24},{24,32},{32,40},{40,48},{48,56},{56,64},{64,7... | collective-permute-start | bytes 589832 | tf_op jit(solution)/shard_map/ppermute | solution.py:21
  42.5 10.6 %collective-permute-start.1 = (f32[192,256]{1,0:T(8,128)S(1)}, f32[192,256]{1,0:T(8,128)S(1)}, u32[]{:S(2)}, u32[]{:S(2)}) collective-permute-start(f32[192,256]{1,0:T(8,128)S(1)} %get-tuple-element.10), channel_id=1, source_target_pairs={{0,504},{8,0},{16,8},{24,16},{32,24},{40,32},{48,40},{56,48},{64,5... | collective-permute-start | bytes 589832 | tf_op jit(solution)/shard_map/ppermute | solution.py:21
  82.4 9.8 %collective-permute-start.2 = (f32[192,256]{1,0:T(8,128)S(1)}, f32[192,256]{1,0:T(8,128)S(1)}, u32[]{:S(2)}, u32[]{:S(2)}) collective-permute-start(f32[192,256]{1,0:T(8,128)S(1)} %get-tuple-element.11), channel_id=1, source_target_pairs={{0,8},{8,16},{16,24},{24,32},{32,40},{40,48},{48,56},{56,64},{64,7... | collective-permute-start | bytes 589832 | tf_op jit(solution)/shard_map/ppermute | solution.py:21
  89.7 8.5 %collective-permute-start.3 = (f32[192,256]{1,0:T(8,128)S(1)}, f32[192,256]{1,0:T(8,128)S(1)}, u32[]{:S(2)}, u32[]{:S(2)}) collective-permute-start(f32[192,256]{1,0:T(8,128)S(1)} %get-tuple-element.12), channel_id=1, source_target_pairs={{0,504},{8,0},{16,8},{24,16},{32,24},{40,32},{48,40},{56,48},{64,5... | collective-permute-start | bytes 589832 | tf_op jit(solution)/shard_map/ppermute | solution.py:21

commit v3 on v2

--- a/solution.py
+++ b/solution.py
@@ -7,17 +7,21 @@
 from jax.experimental.pallas import tpu as pltpu
 from jax.sharding import PartitionSpec as P
 
+
 ROUNDS = 2
 
 
 EPS = 1e-06
 
-ROW_PARTS = 8
+
+def swapped_near(value, axis):
+    count = lax.axis_size(axis)
+    return lax.ppermute(value, axis, [(i, i ^ 1) for i in range(count)])
 
 
-def shifted(value, axis, steps):
+def swapped_far(value, axis):
     count = lax.axis_size(axis)
-    pairs = [(source, (source + steps) % count) for source in range(count)]
+    pairs = [(i, (i + (1 if i % 2 else -1)) % count) for i in range(count)]
     return lax.ppermute(value, axis, pairs)
 
 
@@ -92,7 +96,7 @@
 
 
 def polar_kernel(total_rows, turn, side_ref, packed_ref, *refs):
-    *block_refs, fwd_ref, bwd_ref = refs
+    *block_refs, near_ref, far_ref = refs
     parts, rows, width = packed_ref.shape
     gram, diag_blocks = unpack(packed_ref[...].reshape(parts * rows, width))
     size = gram.shape[0]
@@ -124,9 +128,10 @@
     turned = turned + dot3(split(turned), z_s)
     new = 1.5 * first - 0.5 * turned
     half = size // 2
-    kept = side_ref[turn] == 0
-    fwd_ref[...] = jnp.where(kept, new[:, :half], new[:, half:])
-    bwd_ref[...] = jnp.where(kept, new[:, half:], new[:, :half])
+    side = side_ref[turn] if turn else side_ref[turn] ^ (lax.axis_index("pair") % 2)
+    head = (side == 0) == (turn == 0)
+    near_ref[...] = jnp.where(head, new[:, :half], new[:, half:])
+    far_ref[...] = jnp.where(head, new[:, half:], new[:, :half])
 
 
 def vmem(count):
@@ -166,7 +171,7 @@
             compiler_params=room(8),
         )(terms)
         gathered = lax.all_to_all(summed, "rows", 0, 0)
-        forward, backward = pl.pallas_call(
+        near, far = pl.pallas_call(
             functools.partial(polar_kernel, float(total_rows), turn),
             out_shape=(half_shape, half_shape),
             in_specs=[pl.BlockSpec(memory_space=pltpu.SMEM)] + vmem(1 + len(blocks)),
@@ -174,8 +179,11 @@
             name="polar",
             compiler_params=room(24),
         )(sides, gathered, *blocks)
-        blocks = (shifted(forward, "pair", 1), shifted(backward, "pair", -1))
-    return jnp.concatenate(blocks, axis=1)
+        far = swapped_far(far, "pair")
+        near = swapped_near(near, "pair")
+        blocks = (near, far)
+    odd = lax.axis_index("pair") % 2 == 1
+    return jnp.where(odd, jnp.concatenate((near, far), axis=1), jnp.concatenate((far, near), axis=1))
 
 
 def solution(mesh):

time: 101 us -> 101 us (level); the launches traced: 98.9 us -> 100 us
  starting transfers between devices: 22 us -> 34.2 us
  waiting for transfers between devices: 15.2 us -> 5.72 us
  blocking collectives: 48.4 us -> 47 us
    ppermute x4, starting transfers between devices: 22 us -> 34.2 us  [the longest x2 19.7 us: swapped_near(): return lax.ppermute(value, axis, [(i, i ^ 1) for i in range(count)])]
    ppermute x4, waiting for transfers between devices: 15.2 us -> 5.72 us  [the longest x2 4.69 us: swapped_far(): return lax.ppermute(value, axis, pairs)]
    all_to_all x2, blocking collectives: 26.2 us -> 24.2 us  [local(): terms = lax.all_to_all(partial, 'rows', 0, 0)]
  transfers between devices with their start and end apart: 4 -> 4, of which waited for: 4 -> 2; matrix products, arithmetic and copies ran while one was open for 0% -> 0% of each run, Pallas kernels for 0% -> 0%
where the time goes in v3:
time: 101 us; the launch traced here: 100 us
  blocking collectives  47 us (47%)
  starting transfers between devices  34.2 us (34%)
  Pallas kernels  10.7 us (11%)
  waiting for transfers between devices  5.72 us (6%)
  local copies, waits for them, and re-layouts  1.65 us (2%)
    all_to_all x2, blocking collectives, local(): terms = lax.all_to_all(partial, 'rows', 0, 0)  24.2 us
    all_to_all x2, blocking collectives, local(): gathered = lax.all_to_all(summed, 'rows', 0, 0)  22.9 us
    ppermute x2, starting transfers between devices, swapped_near(): return lax.ppermute(value, axis, [(i, i ^ 1) for i in range(count)])  19.7 us
    ppermute x2, starting transfers between devices, swapped_far(): return lax.ppermute(value, axis, pairs)  14.5 us
    pallas_call x2, Pallas kernels, local(): pl.pallas_call(functools.partial(polar_kernel, float(total_rows), turn),...  9.6 us
    ppermute x2, waiting for transfers between devices, swapped_far(): return lax.ppermute(value, axis, pairs)  4.69 us
  transfers between devices with their start and end apart: 4, of which 2 were waited for; matrix products, arithmetic and copies ran while one was open for 0% of the time, Pallas kernels for 0%

profile of v3, /device:TPU:1, one launch (start us, length us, event | category | flops | bytes accessed | tf_op | source)
XLA Modules:
  0.0 100.2 jit_solution(13075399535131983557)
XLA Ops:
  0.0 0.0 copy-start
  0.0 1.0 copy-done
  1.0 0.5 gram.2
  1.5 13.7 %all_to_all.20.in_ref = f32[8,16,1280]{2,1,0:T(8,128)S(1)} all-to-all(f32[8,16,1280]{2,1,0:T(8,128)S(1)} %gram.2), channel_id=1, replica_groups=mesh['pair'=64,'rows'=8] {'rows'}, dimensions={0} | all-to-all | bytes 1310720 | tf_op jit(solution)/shard_map/all_to_all | solution.py:164
  15.2 0.1 sum.2
  15.3 0.0 copy-start.1
  15.3 10.8 %all_to_all.21.packed_ref = f32[8,16,1280]{2,1,0:T(8,128)S(1)} all-to-all(f32[8,16,1280]{2,1,0:T(8,128)S(1)} %sum.2), channel_id=1, replica_groups=mesh['pair'=64,'rows'=8] {'rows'}, dimensions={0} | all-to-all | bytes 1310720 | tf_op jit(solution)/shard_map/all_to_all | solution.py:173
  26.1 0.0 copy-start.2
  26.1 0.0 copy-done.1
  26.1 0.7 copy-done.2
  26.7 4.8 %polar.2 = (f32[192,256]{1,0:T(8,128)S(1)}, f32[192,256]{1,0:T(8,128)S(1)}) custom-call(s32[2]{0:T(128)S(1)} %bitcast.1, f32[8,16,1280]{2,1,0:T(8,128)S(1)} %all_to_all.21.packed_ref, f32[192,512]{1,0:T(8,128)S(1)} %copy-done.1), custom_call_target="tpu_custom_call" | custom-call | tf_op jit(solution)/shard_map/polar/pallas_call | solution.py:174
  31.5 7.9 %collective-permute-start = (f32[192,256]{1,0:T(8,128)S(1)}, f32[192,256]{1,0:T(8,128)S(1)}, u32[]{:S(2)}, u32[]{:S(2)}) collective-permute-start(f32[192,256]{1,0:T(8,128)S(1)} %get-tuple-element.9), channel_id=1, source_target_pairs={{0,8},{8,0},{16,24},{24,16},{32,40},{40,32},{48,56},{56,48},{64,72... | collective-permute-start | bytes 589832 | tf_op jit(solution)/shard_map/ppermute | solution.py:19
  39.5 4.9 %collective-permute-start.1 = (f32[192,256]{1,0:T(8,128)S(1)}, f32[192,256]{1,0:T(8,128)S(1)}, u32[]{:S(2)}, u32[]{:S(2)}) collective-permute-start(f32[192,256]{1,0:T(8,128)S(1)} %get-tuple-element.10), channel_id=1, source_target_pairs={{0,504},{8,16},{16,8},{24,32},{32,24},{40,48},{48,40},{56,64},{64,... | collective-permute-start | bytes 589832 | tf_op jit(solution)/shard_map/ppermute | solution.py:25
  44.4 0.0 collective-permute-done.refs_0_
  44.4 4.7 %collective-permute-done.1.refs_1_ = f32[192,256]{1,0:T(8,128)S(1)} collective-permute-done((f32[192,256]{1,0:T(8,128)S(1)}, f32[192,256]{1,0:T(8,128)S(1)}, u32[]{:S(2)}, u32[]{:S(2)}) %collective-permute-start.1) | collective-permute-done | bytes 196640 | tf_op jit(solution)/shard_map/ppermute | solution.py:25
  49.1 0.5 gram.3
  49.6 10.5 %all_to_all.22.in_ref = f32[8,16,1280]{2,1,0:T(8,128)S(1)} all-to-all(f32[8,16,1280]{2,1,0:T(8,128)S(1)} %gram.3), channel_id=1, replica_groups=mesh['pair'=64,'rows'=8] {'rows'}, dimensions={0} | all-to-all | bytes 1310720 | tf_op jit(solution)/shard_map/all_to_all | solution.py:164
  60.1 0.1 sum.3
  60.1 12.1 %all_to_all.23.packed_ref = f32[8,16,1280]{2,1,0:T(8,128)S(1)} all-to-all(f32[8,16,1280]{2,1,0:T(8,128)S(1)} %sum.3), channel_id=1, replica_groups=mesh['pair'=64,'rows'=8] {'rows'}, dimensions={0} | all-to-all | bytes 1310720 | tf_op jit(solution)/shard_map/all_to_all | solution.py:173
  72.2 4.8 %polar.3 = (f32[192,256]{1,0:T(8,128)S(1)}, f32[192,256]{1,0:T(8,128)S(1)}) custom-call(s32[2]{0:T(128)S(1)} %bitcast.2, f32[8,16,1280]{2,1,0:T(8,128)S(1)} %all_to_all.23.packed_ref, f32[192,256]{1,0:T(8,128)S(1)} %collective-permute-done.refs_0_, f32[192,256]{1,0:T(8,128)S(1)} %collective-permute-done.1.refs_1_), custom_call_target="tpu_custom_call" | custom-call | tf_op jit(solution)/shard_map/polar/pallas_call | solution.py:174
  77.1 9.6 %collective-permute-start.3 = (f32[192,256]{1,0:T(8,128)S(1)}, f32[192,256]{1,0:T(8,128)S(1)}, u32[]{:S(2)}, u32[]{:S(2)}) collective-permute-start(f32[192,256]{1,0:T(8,128)S(1)} %get-tuple-element.12), channel_id=1, source_target_pairs={{0,504},{8,16},{16,8},{24,32},{32,24},{40,48},{48,40},{56,64},{64,... | collective-permute-start | bytes 589832 | tf_op jit(solution)/shard_map/ppermute | solution.py:25
  86.7 11.7 %collective-permute-start.2 = (f32[192,256]{1,0:T(8,128)S(1)}, f32[192,256]{1,0:T(8,128)S(1)}, u32[]{:S(2)}, u32[]{:S(2)}) collective-permute-start(f32[192,256]{1,0:T(8,128)S(1)} %get-tuple-element.11), channel_id=1, source_target_pairs={{0,8},{8,0},{16,24},{24,16},{32,40},{40,32},{48,56},{56,48},{64,72... | collective-permute-start | bytes 589832 | tf_op jit(solution)/shard_map/ppermute | solution.py:19
  98.4 0.0 collective-permute-done.3
  98.4 1.0 %collective-permute-done.2 = f32[192,256]{1,0:T(8,128)S(1)} collective-permute-done((f32[192,256]{1,0:T(8,128)S(1)}, f32[192,256]{1,0:T(8,128)S(1)}, u32[]{:S(2)}, u32[]{:S(2)}) %collective-permute-start.2) | collective-permute-done | bytes 196640 | tf_op jit(solution)/shard_map/ppermute | solution.py:19
  99.4 0.8 maximum_select_fusion
Async XLA Ops:
  0.0 1.0 copy-start
  15.3 10.8 %copy-start.1 = (f32[192,512]{1,0:T(8,128)S(1)}, f32[192,512]{1,0:T(8,128)}, u32[]{:S(2)}) copy-start(f32[192,512]{1,0:T(8,128)} %refs_0_.3) | copy-start | bytes 1179652
  26.1 0.7 copy-start.2
  31.5 12.9 %collective-permute-start = (f32[192,256]{1,0:T(8,128)S(1)}, f32[192,256]{1,0:T(8,128)S(1)}, u32[]{:S(2)}, u32[]{:S(2)}) collective-permute-start(f32[192,256]{1,0:T(8,128)S(1)} %get-tuple-element.9), channel_id=1, source_target_pairs={{0,8},{8,0},{16,24},{24,16},{32,40},{40,32},{48,56},{56,48},{64,72... | collective-permute-start | bytes 589832 | tf_op jit(solution)/shard_map/ppermute | solution.py:19
  39.5 9.6 %collective-permute-start.1 = (f32[192,256]{1,0:T(8,128)S(1)}, f32[192,256]{1,0:T(8,128)S(1)}, u32[]{:S(2)}, u32[]{:S(2)}) collective-permute-start(f32[192,256]{1,0:T(8,128)S(1)} %get-tuple-element.10), channel_id=1, source_target_pairs={{0,504},{8,16},{16,8},{24,32},{32,24},{40,48},{48,40},{56,64},{64,... | collective-permute-start | bytes 589832 | tf_op jit(solution)/shard_map/ppermute | solution.py:25
  77.1 21.4 %collective-permute-start.3 = (f32[192,256]{1,0:T(8,128)S(1)}, f32[192,256]{1,0:T(8,128)S(1)}, u32[]{:S(2)}, u32[]{:S(2)}) collective-permute-start(f32[192,256]{1,0:T(8,128)S(1)} %get-tuple-element.12), channel_id=1, source_target_pairs={{0,504},{8,16},{16,8},{24,32},{32,24},{40,48},{48,40},{56,64},{64,... | collective-permute-start | bytes 589832 | tf_op jit(solution)/shard_map/ppermute | solution.py:25
  86.7 12.8 %collective-permute-start.2 = (f32[192,256]{1,0:T(8,128)S(1)}, f32[192,256]{1,0:T(8,128)S(1)}, u32[]{:S(2)}, u32[]{:S(2)}) collective-permute-start(f32[192,256]{1,0:T(8,128)S(1)} %get-tuple-element.11), channel_id=1, source_target_pairs={{0,8},{8,0},{16,24},{24,16},{32,40},{40,32},{48,56},{56,48},{64,72... | collective-permute-start | bytes 589832 | tf_op jit(solution)/shard_map/ppermute | solution.py:19

commit v4 on v3

v4 whole, which is shorter than its diff:
```python
import functools

import jax
import jax.numpy as jnp
from jax import lax
from jax.experimental import pallas as pl
from jax.experimental.pallas import tpu as pltpu
from jax.sharding import PartitionSpec as P


ROUNDS = 2


EPS = 1e-06


def swapped_near(value, axis):
    count = lax.axis_size(axis)
    return lax.ppermute(value, axis, [(i, i ^ 1) for i in range(count)])


def swapped_far(value, axis):
    count = lax.axis_size(axis)
    pairs = [(i, (i + (1 if i % 2 else -1)) % count) for i in range(count)]
    return lax.ppermute(value, axis, pairs)


def split(value):
    high = value.astype(jnp.bfloat16)
    return high, (value - high.astype(jnp.float32)).astype(jnp.bfloat16)


def dot(left, right):
    return jnp.dot(left, right, preferred_element_type=jnp.float32)


def dot3(left, right):
    left_high, left_low = left
    right_high, right_low = right
    small = dot(left_high, right_low) + dot(left_low, right_high)
    return dot(left_high, right_high) + small


def joined(refs):
    return jnp.concatenate([ref[...] for ref in refs], axis=1)


def gram_kernel(*refs):
    *block_refs, out_ref = refs
    block = joined(block_refs)
    half = block.shape[1] // 2
    mid = half // 2
    whole = split(block)
    left_t = split(block[:, :half].T)
    right_t = split(block[:, half:].T)
    upper = dot3(left_t, whole)
    lower = dot3(right_t, (whole[0][:, half:], whole[1][:, half:]))
    parts = out_ref.shape[0]
    rows = mid // parts
    spots = (
        upper[:mid, :half],
        upper[mid:, mid:half],
        lower[:mid],
        lower[mid:, mid:],
        upper[:mid, half:],
        upper[mid:, half:],
    )
    start = 0
    for spot in spots:
        width = spot.shape[1]
        out_ref[:, :, start : start + width] = spot.reshape(parts, rows, width)
        start += width


def corner_kernel(near_ref, far_ref, out_ref):
    parts, rows, width = out_ref.shape
    half = width // 2
    count = near_ref.shape[0] - 3 * half // 4
    near_t = split(near_ref[:count].T)
    corner = dot3(near_t, split(far_ref[:count]))
    mid = parts * rows
    out_ref[:, :, :half] = corner[:mid].reshape(parts, rows, half)
    out_ref[:, :, half:] = corner[mid:].reshape(parts, rows, half)


def sum_kernel(*refs):
    *far_refs, in_ref, out_ref = refs
    parts, rows, _ = in_ref.shape
    total = in_ref[0]
    for part in range(1, parts):
        total = total + in_ref[part]
    pieces = [total]
    for far_ref in far_refs:
        half = far_ref.shape[1]
        mid = half // 2
        start = far_ref.shape[0] - 3 * rows // 2
        pieces.append(far_ref[start : start + rows])
        tail = far_ref[start + rows :]
        pieces.append(jnp.concatenate([tail[:, :mid], tail[:, mid:]], axis=0))
    total = jnp.concatenate(pieces, axis=1)
    for part in range(parts):
        out_ref[part] = total


CHUNK = 32


def put(value, store):
    for start in range(0, value.shape[0], CHUNK):
        store(slice(start, start + CHUNK), value[start : start + CHUNK])


MATRICES = 5
PAIRS = 7


def polar_scratch(rows, size):
    return (
        [pltpu.VMEM((size, size), jnp.float32)] * MATRICES
        + [pltpu.VMEM((size, size), jnp.bfloat16)] * (2 * PAIRS)
        + [pltpu.VMEM((4, rows, size), jnp.float32)]
        + [pltpu.VMEM((4, rows, size), jnp.bfloat16)] * 2
        + [pltpu.VMEM((size // 2, size // 2), jnp.float32)]
    )


def polar_kernel(total_rows, turn, side_ref, packed_ref, *refs):
    scratch = len(polar_scratch(8, 8))
    *block_refs, near_ref, far_ref = refs[:-scratch]
    refs = refs[-scratch:]
    dev, two, zed, bee, sqr = refs[:MATRICES]
    pairs = refs[MATRICES : MATRICES + 2 * PAIRS]
    dev_s, two_s, mix_s, zed_s, dub_s, bee_s, sqr_s = zip(pairs[::2], pairs[1::2])
    val, val_h, val_l, far_diag = refs[MATRICES + 2 * PAIRS :]
    opening, closing = turn == 0, turn == ROUNDS - 1
    parts, part_rows, _ = packed_ref.shape
    mid = parts * part_rows
    half = 2 * mid
    size = 2 * half
    count = val.shape[1]
    low, high = slice(0, half), slice(half, size)
    halves = (low, high)
    whole = slice(0, size)

    def at(i):
        return slice(i * mid, (i + 1) * mid)

    places = ((0, 0), (1, 1), (2, 2), (3, 3), (0, 1), (2, 3), (0, 2), (0, 3), (1, 2), (1, 3))
    spots = (0, 2, 3, 5, 1, 4, 6, 7, 8, 9) if opening else (-1, -1, 4, 6, -1, 5, 0, 1, 2, 3)
    eye = lax.broadcasted_iota(jnp.int32, (mid, mid), 0) == lax.broadcasted_iota(
        jnp.int32, (mid, mid), 1
    )
    one = jnp.where(eye, 1.0, 0.0)

    def gram_at(place):
        spot = spots[places.index(place)]
        if spot >= 0:
            return packed_ref[:, :, at(spot)].reshape(mid, mid)
        near = block_refs[0]
        if place[0] == 0:
            return near[count : count + mid, at(place[1])]
        return jnp.concatenate([near[count + mid :, at(0)], near[count + mid :, at(1)]], axis=0)

    along, down = [], []
    for i in range(4):
        total = jnp.sum(jnp.where(eye, gram_at((i, i)), 0.0), axis=0, keepdims=True)
        along.append(lax.rsqrt(total + EPS * total_rows))
        down.append(jnp.broadcast_to(along[i], (mid, mid)).T)
    square = jnp.zeros((8, mid), jnp.float32)
    square_off = jnp.zeros((8, mid), jnp.float32)
    for i, j in places:
        corr = gram_at((i, j)) * down[i] * along[j]
        term = jnp.sum((corr * corr).reshape(mid // 8, 8, mid), axis=0)
        if i == j:
            square = square + term
            corr = corr - one
        else:
            square_off = square_off + term
        for row, column, value in ((i, j, corr),) if i == j else ((i, j, corr), (j, i, corr.T)):
            dev[at(row), at(column)] = value
            dev_s[0][at(row), at(column)], dev_s[1][at(row), at(column)] = split(value)
    square = square + 2.0 * square_off
    square = jnp.sum(jnp.sum(square, axis=0, keepdims=True), axis=1, keepdims=True)
    s = lax.rsqrt(square / size)
    t = s - 1.0
    c_four = 0.0625 * s * s * s * s
    c_three = s * s * s * (0.25 * t - 0.3125)
    c_two = s * s * (0.375 + t * (0.375 * t - 0.9375))
    c_one = s * (t * (0.75 + t * (0.25 * t - 0.9375)) - 0.5)
    c_zero = 1.0 + t * (t * (0.375 + t * (0.0625 * t - 0.3125)) - 0.5)

    def times(row, left, right, column):
        return dot3((left[0][row], left[1][row]), (right[0][:, column], right[1][:, column]))

    def symmetric(left, right, store, mirrored):
        for column, row in ((high, whole), (low, low)):

            def keep(piece, value):
                store(piece, column, value)

            put(times(row, left, right, column), keep)
            if row == whole:
                for ref in mirrored:
                    ref[high, low] = ref[low, high].T

    def put_split(pair, piece, column, value):
        pair[0][piece, column], pair[1][piece, column] = split(value)

    def keep_two(piece, column, value):
        two[piece, column] = value
        put_split(two_s, piece, column, value)
        put_split(mix_s, piece, column, c_four * value + c_three * dev[piece, column])

    def keep_zed(piece, column, value):
        value = value + c_two * two[piece, column] + c_one * dev[piece, column]
        zed[piece, column] = value
        put_split(zed_s, piece, column, value)

    def keep_dub(piece, column, value):
        value = value + (2.0 * c_zero) * zed[piece, column]
        two[piece, column] = s * value + (s * c_zero * c_zero) * dev[piece, column]
        put_split(dub_s, piece, column, s * value)

    def keep_bee(piece, column, value):
        value = value + two[piece, column]
        rows = lax.broadcasted_iota(jnp.int32, value.shape, 0) + piece.start
        columns = lax.broadcasted_iota(jnp.int32, value.shape, 1) + column.start
        value = value + jnp.where(rows == columns, s * c_zero * c_zero - 1.0, 0.0)
        bee[piece, column] = value
        put_split(bee_s, piece, column, value)

    def keep_sqr(piece, column, value):
        sqr[piece, column] = value
        put_split(sqr_s, piece, column, value)

    symmetric(dev_s, dev_s, keep_two, two_s + mix_s)
    symmetric(two_s, mix_s, keep_zed, zed_s)

    def keep_val(step):
        def store(piece, value):
            val[step, piece] = value
            val_h[step, piece], val_l[step, piece] = split(value)

        return store

    block = jnp.concatenate([ref[:count] for ref in block_refs], axis=1)
    put(block * jnp.concatenate(along, axis=1), keep_val(0))
    norm = jnp.sqrt(total_rows * s)
    side = side_ref[turn] if turn else side_ref[turn] ^ (lax.axis_index("pair") % 2)
    head = (side == 0) == opening
    if closing:
        plan = ((zed_s, c_zero), (dev_s, 1.0), (zed_s, c_zero), (zed_s, c_zero))
        mine, other = 1.5 * norm, -0.5 * norm * s
    else:
        plan = ((zed_s, c_zero), (bee_s, 0.0))
        mine, other = norm, -0.5 * norm
    for step, (right, factor) in enumerate(plan):
        if right is bee_s:
            symmetric(zed_s, zed_s, keep_dub, dub_s)
            symmetric(dev_s, dub_s, keep_bee, bee_s)
        new = []
        for column in halves:
            product = times(slice(None), (val_h.at[step], val_l.at[step]), right, column)

            def store(piece, value):
                if right is not bee_s:
                    value = value + factor * val[step, piece, column]
                if step == len(plan) - 1:
                    new.append(mine * val[1, piece, column] + other * value)
                else:
                    val[step + 1, piece, column] = value
                    val_h[step + 1, piece, column], val_l[step + 1, piece, column] = split(value)

            put(product, store)
    steps = len(new) // 2
    for k in range(steps):
        piece = slice(k * CHUNK, (k + 1) * CHUNK)
        near_ref[piece] = jnp.where(head, new[k], new[steps + k])
        far_ref[piece] = jnp.where(head, new[steps + k], new[k])
    if closing:
        return
    symmetric(bee_s, bee_s, keep_sqr, sqr_s)
    grams = []
    for column in halves:
        gram = []

        def keep_gram(piece, value):
            piece_in = slice(piece.start + column.start, piece.stop + column.start)
            value = 0.25 * value - 0.75 * sqr[piece_in, column]
            rows = lax.broadcasted_iota(jnp.int32, value.shape, 0) + piece.start
            columns = lax.broadcasted_iota(jnp.int32, value.shape, 1)
            gram.append(total_rows * (value + jnp.where(rows == columns, 1.0, 0.0)))

        put(times(column, sqr_s, bee_s, column), keep_gram)
        grams.append(gram)
    steps = len(grams[0])
    for k in range(steps):
        start = k * CHUNK
        near = jnp.where(head, grams[0][k], grams[1][k])
        far_diag[start : start + CHUNK] = jnp.where(head, grams[1][k], grams[0][k])
        if start < mid:
            near_ref[count + start : count + start + CHUNK] = near
        else:
            into, column = (start - mid) % (mid // 2), at((start - mid) // (mid // 2))
            into = count + mid + into
            near_ref[into : into + CHUNK, column] = near[:, mid:]
    spot = lax.axis_index("rows") * part_rows
    top = far_diag[pl.ds(pl.multiple_of(spot, 8), part_rows)]
    bottom = far_diag[pl.ds(pl.multiple_of(spot + mid, 8), part_rows)][:, mid:]
    far_ref[count : count + part_rows] = top
    far_ref[count + part_rows :, :mid] = bottom[: part_rows // 2]
    far_ref[count + part_rows :, mid:] = bottom[part_rows // 2 :]


def vmem(count):
    return [pl.BlockSpec(memory_space=pltpu.VMEM)] * count


def room(mib):
    return pltpu.CompilerParams(vmem_limit_bytes=mib * 2**20)


def local(snapshot, keep_side):
    parts = lax.axis_size("rows")
    rows, size = snapshot.shape
    total_rows = rows * parts
    half = size // 2
    mid = half // 2
    blocks = (snapshot,)
    sides = keep_side.reshape(keep_side.shape[0])
    part_rows = mid // parts

    def shape(*sizes):
        return jax.ShapeDtypeStruct(sizes, jnp.float32)

    for turn in range(ROUNDS):
        extra = turn < ROUNDS - 1
        sent = 10 * mid if turn == 0 else 4 * mid
        partial = pl.pallas_call(
            corner_kernel if turn else gram_kernel,
            out_shape=shape(parts, part_rows, sent),
            in_specs=vmem(len(blocks)),
            out_specs=vmem(1)[0],
            name="gram",
            compiler_params=room(8),
        )(*blocks)
        terms = lax.all_to_all(partial, "rows", 0, 0)
        slices = blocks[1:]
        summed = pl.pallas_call(
            sum_kernel,
            out_shape=shape(parts, part_rows, sent + 3 * mid * len(slices)),
            in_specs=vmem(1 + len(slices)),
            out_specs=vmem(1)[0],
            name="sum",
            compiler_params=room(8),
        )(*slices, terms)
        gathered = lax.all_to_all(summed, "rows", 0, 0)
        near_rows = rows + extra * 3 * mid // 2
        far_rows = rows + extra * 3 * part_rows // 2
        near, far = pl.pallas_call(
            functools.partial(polar_kernel, float(total_rows), turn),
            out_shape=(shape(near_rows, half), shape(far_rows, half)),
            in_specs=[pl.BlockSpec(memory_space=pltpu.SMEM)] + vmem(1 + len(blocks)),
            out_specs=tuple(vmem(2)),
            scratch_shapes=polar_scratch(rows, size),
            name="polar",
            compiler_params=room(24),
        )(sides, gathered, *blocks)
        far = swapped_far(far, "pair")
        near = swapped_near(near, "pair")
        blocks = (near, far)
    odd = lax.axis_index("pair") % 2 == 1
    return jnp.where(odd, jnp.concatenate((near, far), axis=1), jnp.concatenate((far, near), axis=1))


def solution(mesh):
    placed = (P("rows", "pair"), P(None, "pair"))
    return jax.shard_map(
        local, mesh=mesh, in_specs=placed, out_specs=P("rows", "pair"), check_vma=False
    )
```

time: 101 us -> 95.4 us (0.945)
  starting transfers between devices: 34.2 us -> 30.2 us
  blocking collectives: 47 us -> 43.5 us
    all_to_all x2, blocking collectives: 24.2 us -> 21.9 us  [local(): terms = lax.all_to_all(partial, 'rows', 0, 0)]
    ppermute x2, starting transfers between devices: 14.5 us -> 12.3 us  [swapped_far(): return lax.ppermute(value, axis, pairs)]
    ppermute x2, starting transfers between devices: 19.7 us -> 17.9 us  [swapped_near(): return lax.ppermute(value, axis, [(i, i ^ 1) for i in range(count)])]
    all_to_all x2, blocking collectives: 22.9 us -> 21.6 us  [local(): gathered = lax.all_to_all(summed, 'rows', 0, 0)]
    pallas_call x2, Pallas kernels: 9.6 us -> 10.8 us  [local(): pl.pallas_call(functools.partial(polar_kernel, float(total_rows), turn),...]
where the time goes in v4:
time: 95.4 us; the launch traced here: 94.3 us
  blocking collectives  43.5 us (46%)
  starting transfers between devices  30.2 us (32%)
  Pallas kernels  11.7 us (12%)
  waiting for transfers between devices  6.26 us (7%)
  local copies, waits for them, and re-layouts  1.65 us (2%)
    all_to_all x2, blocking collectives, local(): terms = lax.all_to_all(partial, 'rows', 0, 0)  21.9 us
    all_to_all x2, blocking collectives, local(): gathered = lax.all_to_all(summed, 'rows', 0, 0)  21.6 us
    ppermute x2, starting transfers between devices, swapped_near(): return lax.ppermute(value, axis, [(i, i ^ 1) for i in range(count)])  17.9 us
    ppermute x2, starting transfers between devices, swapped_far(): return lax.ppermute(value, axis, pairs)  12.3 us
    pallas_call x2, Pallas kernels, local(): pl.pallas_call(functools.partial(polar_kernel, float(total_rows), turn),...  10.8 us
    ppermute x2, waiting for transfers between devices, swapped_far(): return lax.ppermute(value, axis, pairs)  5.23 us
  transfers between devices with their start and end apart: 4, of which 2 were waited for; matrix products, arithmetic and copies ran while one was open for 0% of the time, Pallas kernels for 0%

profile of v4, /device:TPU:1, one launch (start us, length us, event | category | flops | bytes accessed | tf_op | source)
XLA Modules:
  0.0 94.3 jit_solution(421977587971292020)
XLA Ops:
  0.0 0.0 copy-start
  0.0 1.0 %copy-done = f32[192,512]{1,0:T(8,128)S(1)} copy-done((f32[192,512]{1,0:T(8,128)S(1)}, f32[192,512]{1,0:T(8,128)}, u32[]{:S(2)}) %copy-start) | copy-done | bytes 393240
  1.0 0.5 gram.2
  1.5 13.7 %all_to_all.20.refs_0_ = f32[8,16,1280]{2,1,0:T(8,128)S(1)} all-to-all(f32[8,16,1280]{2,1,0:T(8,128)S(1)} %gram.2), channel_id=1, replica_groups=mesh['pair'=64,'rows'=8] {'rows'}, dimensions={0} | all-to-all | bytes 1310720 | tf_op jit(solution)/shard_map/all_to_all | solution.py:347
  15.2 0.1 sum.2
  15.3 0.0 copy-start.1
  15.3 10.8 %all_to_all.21.packed_ref = f32[8,16,1280]{2,1,0:T(8,128)S(1)} all-to-all(f32[8,16,1280]{2,1,0:T(8,128)S(1)} %sum.2), channel_id=1, replica_groups=mesh['pair'=64,'rows'=8] {'rows'}, dimensions={0} | all-to-all | bytes 1310720 | tf_op jit(solution)/shard_map/all_to_all | solution.py:357
  26.1 0.0 copy-start.2
  26.1 0.0 copy-done.1
  26.1 0.7 copy-done.2
  26.7 6.4 %polar.2 = (f32[384,256]{1,0:T(8,128)S(1)}, f32[216,256]{1,0:T(8,128)S(1)}) custom-call(s32[2]{0:T(128)S(1)} %bitcast.1, f32[8,16,1280]{2,1,0:T(8,128)S(1)} %all_to_all.21.packed_ref, f32[192,512]{1,0:T(8,128)S(1)} %copy-done.1), custom_call_target="tpu_custom_call" | custom-call | tf_op jit(solution)/shard_map/polar/pallas_call | solution.py:360
  33.1 7.9 %collective-permute-start.1 = (f32[384,256]{1,0:T(8,128)S(1)}, f32[384,256]{1,0:T(8,128)S(1)}, u32[]{:S(2)}, u32[]{:S(2)}) collective-permute-start(f32[384,256]{1,0:T(8,128)S(1)} %get-tuple-element.10), channel_id=1, source_target_pairs={{0,8},{8,0},{16,24},{24,16},{32,40},{40,32},{48,56},{56,48},{64,72... | collective-permute-start | bytes 1179656 | tf_op jit(solution)/shard_map/ppermute | solution.py:19
  41.1 4.9 %collective-permute-start = (f32[216,256]{1,0:T(8,128)S(1)}, f32[216,256]{1,0:T(8,128)S(1)}, u32[]{:S(2)}, u32[]{:S(2)}) collective-permute-start(f32[216,256]{1,0:T(8,128)S(1)} %get-tuple-element.9), channel_id=1, source_target_pairs={{0,504},{8,16},{16,8},{24,32},{32,24},{40,48},{48,40},{56,64},{64,... | collective-permute-start | bytes 663560 | tf_op jit(solution)/shard_map/ppermute | solution.py:25
  46.0 5.2 %collective-permute-done.far_ref.refs_0_.refs_1_ = f32[216,256]{1,0:T(8,128)S(1)} collective-permute-done((f32[216,256]{1,0:T(8,128)S(1)}, f32[216,256]{1,0:T(8,128)S(1)}, u32[]{:S(2)}, u32[]{:S(2)}) %collective-permute-start) | collective-permute-done | bytes 221216 | tf_op jit(solution)/shard_map/ppermute | solution.py:25
  51.2 0.0 collective-permute-done.1.near_ref.refs_0_
  51.2 0.3 gram.3
  51.6 8.2 %all_to_all.22.refs_1_ = f32[8,16,512]{2,1,0:T(8,128)S(1)} all-to-all(f32[8,16,512]{2,1,0:T(8,128)S(1)} %gram.3), channel_id=1, replica_groups=mesh['pair'=64,'rows'=8] {'rows'}, dimensions={0} | all-to-all | bytes 524288 | tf_op jit(solution)/shard_map/all_to_all | solution.py:347
  59.8 10.9 %all_to_all.23.packed_ref = f32[8,16,896]{2,1,0:T(8,128)S(1)} all-to-all(f32[8,16,896]{2,1,0:T(8,128)S(1)} %sum.3), channel_id=1, replica_groups=mesh['pair'=64,'rows'=8] {'rows'}, dimensions={0} | all-to-all | bytes 917504 | tf_op jit(solution)/shard_map/all_to_all | solution.py:357
  70.7 4.4 %polar.3 = (f32[192,256]{1,0:T(8,128)S(1)}, f32[192,256]{1,0:T(8,128)S(1)}) custom-call(s32[2]{0:T(128)S(1)} %bitcast.2, f32[8,16,896]{2,1,0:T(8,128)S(1)} %all_to_all.23.packed_ref, f32[384,256]{1,0:T(8,128)S(1)} %collective-permute-done.1.near_ref.refs_0_, f32[216,256]{1,0:T(8,128)S(1)} %collective-permute-done.far_ref.refs_0_.refs_1_), custom_call_target="tpu_custom_call" | custom-call | tf_op jit(solution)/shard_map/polar/pallas_call | solution.py:360
  75.0 7.4 %collective-permute-start.3 = (f32[192,256]{1,0:T(8,128)S(1)}, f32[192,256]{1,0:T(8,128)S(1)}, u32[]{:S(2)}, u32[]{:S(2)}) collective-permute-start(f32[192,256]{1,0:T(8,128)S(1)} %get-tuple-element.12), channel_id=1, source_target_pairs={{0,504},{8,16},{16,8},{24,32},{32,24},{40,48},{48,40},{56,64},{64,... | collective-permute-start | bytes 589832 | tf_op jit(solution)/shard_map/ppermute | solution.py:25
  82.5 10.0 %collective-permute-start.2 = (f32[192,256]{1,0:T(8,128)S(1)}, f32[192,256]{1,0:T(8,128)S(1)}, u32[]{:S(2)}, u32[]{:S(2)}) collective-permute-start(f32[192,256]{1,0:T(8,128)S(1)} %get-tuple-element.11), channel_id=1, source_target_pairs={{0,8},{8,0},{16,24},{24,16},{32,40},{40,32},{48,56},{56,48},{64,72... | collective-permute-start | bytes 589832 | tf_op jit(solution)/shard_map/ppermute | solution.py:19
  92.5 0.0 collective-permute-done.3
  92.5 1.0 %collective-permute-done.2 = f32[192,256]{1,0:T(8,128)S(1)} collective-permute-done((f32[192,256]{1,0:T(8,128)S(1)}, f32[192,256]{1,0:T(8,128)S(1)}, u32[]{:S(2)}, u32[]{:S(2)}) %collective-permute-start.2) | collective-permute-done | bytes 196640 | tf_op jit(solution)/shard_map/ppermute | solution.py:19
  93.5 0.8 maximum_select_fusion
  (1 shorter events, 0.0 us)
Async XLA Ops:
  0.0 1.0 %copy-start = (f32[192,512]{1,0:T(8,128)S(1)}, f32[192,512]{1,0:T(8,128)}, u32[]{:S(2)}) copy-start(f32[192,512]{1,0:T(8,128)} %refs_0_.3) | copy-start | bytes 1179652
  15.3 10.8 %copy-start.1 = (f32[192,512]{1,0:T(8,128)S(1)}, f32[192,512]{1,0:T(8,128)}, u32[]{:S(2)}) copy-start(f32[192,512]{1,0:T(8,128)} %refs_0_.3) | copy-start | bytes 1179652
  26.1 0.7 copy-start.2
  33.1 18.1 %collective-permute-start.1 = (f32[384,256]{1,0:T(8,128)S(1)}, f32[384,256]{1,0:T(8,128)S(1)}, u32[]{:S(2)}, u32[]{:S(2)}) collective-permute-start(f32[384,256]{1,0:T(8,128)S(1)} %get-tuple-element.10), channel_id=1, source_target_pairs={{0,8},{8,0},{16,24},{24,16},{32,40},{40,32},{48,56},{56,48},{64,72... | collective-permute-start | bytes 1179656 | tf_op jit(solution)/shard_map/ppermute | solution.py:19
  41.1 10.1 %collective-permute-start = (f32[216,256]{1,0:T(8,128)S(1)}, f32[216,256]{1,0:T(8,128)S(1)}, u32[]{:S(2)}, u32[]{:S(2)}) collective-permute-start(f32[216,256]{1,0:T(8,128)S(1)} %get-tuple-element.9), channel_id=1, source_target_pairs={{0,504},{8,16},{16,8},{24,32},{32,24},{40,48},{48,40},{56,64},{64,... | collective-permute-start | bytes 663560 | tf_op jit(solution)/shard_map/ppermute | solution.py:25
  75.0 17.4 %collective-permute-start.3 = (f32[192,256]{1,0:T(8,128)S(1)}, f32[192,256]{1,0:T(8,128)S(1)}, u32[]{:S(2)}, u32[]{:S(2)}) collective-permute-start(f32[192,256]{1,0:T(8,128)S(1)} %get-tuple-element.12), channel_id=1, source_target_pairs={{0,504},{8,16},{16,8},{24,32},{32,24},{40,48},{48,40},{56,64},{64,... | collective-permute-start | bytes 589832 | tf_op jit(solution)/shard_map/ppermute | solution.py:25
  82.5 11.0 %collective-permute-start.2 = (f32[192,256]{1,0:T(8,128)S(1)}, f32[192,256]{1,0:T(8,128)S(1)}, u32[]{:S(2)}, u32[]{:S(2)}) collective-permute-start(f32[192,256]{1,0:T(8,128)S(1)} %get-tuple-element.11), channel_id=1, source_target_pairs={{0,8},{8,0},{16,24},{24,16},{32,40},{40,32},{48,56},{56,48},{64,72... | collective-permute-start | bytes 589832 | tf_op jit(solution)/shard_map/ppermute | solution.py:19

commit v5 on v4

--- a/solution.py
+++ b/solution.py
@@ -43,6 +43,10 @@
 
 def joined(refs):
     return jnp.concatenate([ref[...] for ref in refs], axis=1)
+
+
+def square_index(size):
+    return tuple(lax.broadcasted_iota(jnp.int32, (size, size), axis) for axis in (0, 1))
 
 
 def gram_kernel(*refs):
@@ -57,13 +61,20 @@
     lower = dot3(right_t, (whole[0][:, half:], whole[1][:, half:]))
     parts = out_ref.shape[0]
     rows = mid // parts
+    row, column = square_index(mid)
+    ends = upper[mid:, mid:half], lower[mid:, mid:]
+    diagonals = jnp.zeros((mid, mid), jnp.float32)
+    for i, end in enumerate(ends):
+        line = jnp.sum(jnp.where(row == column, end, 0.0), axis=0, keepdims=True)
+        diagonals = diagonals + jnp.where(row == i, line, 0.0)
     spots = (
-        upper[:mid, :half],
-        upper[mid:, mid:half],
-        lower[:mid],
-        lower[mid:, mid:],
+        jnp.where(row <= column, upper[:mid, :mid], ends[0]),
+        upper[:mid, mid:half],
+        jnp.where(row <= column, lower[:mid, :mid], ends[1]),
+        lower[:mid, mid:],
         upper[:mid, half:],
         upper[mid:, half:],
+        diagonals,
     )
     start = 0
     for spot in spots:
@@ -110,6 +121,21 @@
         store(slice(start, start + CHUNK), value[start : start + CHUNK])
 
 
+def place_kernel(near_ref, far_ref, out_ref, sems):
+    half = near_ref.shape[1]
+    odd = lax.axis_index("pair") % 2
+    copies = [
+        pltpu.make_async_copy(
+            ref, out_ref.at[:, pl.ds(pl.multiple_of(start * half, half), half)], sems.at[i]
+        )
+        for i, (ref, start) in enumerate(((near_ref, 1 - odd), (far_ref, odd)))
+    ]
+    for copy in copies:
+        copy.start()
+    for copy in copies:
+        copy.wait()
+
+
 MATRICES = 5
 PAIRS = 7
 
@@ -146,16 +172,21 @@
         return slice(i * mid, (i + 1) * mid)
 
     places = ((0, 0), (1, 1), (2, 2), (3, 3), (0, 1), (2, 3), (0, 2), (0, 3), (1, 2), (1, 3))
-    spots = (0, 2, 3, 5, 1, 4, 6, 7, 8, 9) if opening else (-1, -1, 4, 6, -1, 5, 0, 1, 2, 3)
-    eye = lax.broadcasted_iota(jnp.int32, (mid, mid), 0) == lax.broadcasted_iota(
-        jnp.int32, (mid, mid), 1
-    )
+    spots = (0, 0, 2, 2, 1, 3, 4, 5, 6, 7) if opening else (-1, -1, 4, 6, -1, 5, 0, 1, 2, 3)
+    row_at, column_at = square_index(mid)
+    eye = row_at == column_at
     one = jnp.where(eye, 1.0, 0.0)
 
     def gram_at(place):
         spot = spots[places.index(place)]
         if spot >= 0:
-            return packed_ref[:, :, at(spot)].reshape(mid, mid)
+            found = packed_ref[:, :, at(spot)].reshape(mid, mid)
+            if not opening or place[0] != place[1]:
+                return found
+            if place[0] % 2 == 0:
+                return jnp.where(row_at <= column_at, found, found.T)
+            line = packed_ref[0, place[0] // 2 : place[0] // 2 + 1, at(8)]
+            return jnp.where(eye, line, jnp.where(row_at > column_at, found, found.T))
         near = block_refs[0]
         if place[0] == 0:
             return near[count : count + mid, at(place[1])]
@@ -335,7 +366,7 @@
 
     for turn in range(ROUNDS):
         extra = turn < ROUNDS - 1
-        sent = 10 * mid if turn == 0 else 4 * mid
+        sent = 9 * mid if turn == 0 else 4 * mid
         partial = pl.pallas_call(
             corner_kernel if turn else gram_kernel,
             out_shape=shape(parts, part_rows, sent),
@@ -369,8 +400,15 @@
         far = swapped_far(far, "pair")
         near = swapped_near(near, "pair")
         blocks = (near, far)
-    odd = lax.axis_index("pair") % 2 == 1
-    return jnp.where(odd, jnp.concatenate((near, far), axis=1), jnp.concatenate((far, near), axis=1))
+    return pl.pallas_call(
+        place_kernel,
+        out_shape=shape(rows, size),
+        in_specs=vmem(2),
+        out_specs=pl.BlockSpec(memory_space=pltpu.HBM),
+        scratch_shapes=[pltpu.SemaphoreType.DMA((2,))],
+        name="place",
+        compiler_params=room(8),
+    )(*blocks)
 
 
 def solution(mesh):

time: 95.4 us -> 98.1 us (1.028)
  waiting for transfers between devices: 6.26 us -> 13.9 us
  starting transfers between devices: 30.2 us -> 26.3 us
    ppermute x2, waiting for transfers between devices: 5.23 us -> 13.9 us  [swapped_far(): return lax.ppermute(value, axis, pairs)]
    ppermute x2, starting transfers between devices: 12.3 us -> 6.28 us  [swapped_far(): return lax.ppermute(value, axis, pairs)]
    ppermute x2, starting transfers between devices: 17.9 us -> 20 us  [swapped_near(): return lax.ppermute(value, axis, [(i, i ^ 1) for i in range(count)])]
    ppermute x2, waiting for transfers between devices: 1.03 us -> 0.01 us  [swapped_near(): return lax.ppermute(value, axis, [(i, i ^ 1) for i in range(count)])]
where the time goes in v5:
time: 98.1 us; the launch traced here: 97.7 us
  blocking collectives  43.2 us (44%)
  starting transfers between devices  26.3 us (27%)
  waiting for transfers between devices  13.9 us (14%)
  Pallas kernels  12.5 us (13%)
  local copies, waits for them, and re-layouts  1.65 us (2%)
    all_to_all x2, blocking collectives, local(): terms = lax.all_to_all(partial, 'rows', 0, 0)  21.9 us
    all_to_all x2, blocking collectives, local(): gathered = lax.all_to_all(summed, 'rows', 0, 0)  21.4 us
    ppermute x2, starting transfers between devices, swapped_near(): return lax.ppermute(value, axis, [(i, i ^ 1) for i in range(count)])  20 us
    ppermute x2, waiting for transfers between devices, swapped_far(): return lax.ppermute(value, axis, pairs)  13.9 us
    pallas_call x2, Pallas kernels, local(): pl.pallas_call(functools.partial(polar_kernel, float(total_rows), turn),...  10.8 us
    ppermute x2, starting transfers between devices, swapped_far(): return lax.ppermute(value, axis, pairs)  6.28 us
  transfers between devices with their start and end apart: 4, of which 2 were waited for; matrix products, arithmetic and copies ran while one was open for 0% of the time, Pallas kernels for 0%

profile of v5, /device:TPU:1, one launch (start us, length us, event | category | flops | bytes accessed | tf_op | source)
XLA Modules:
  0.0 97.7 jit_solution(12555917919697354728)
XLA Ops:
  0.0 0.0 copy-start
  0.0 1.0 %copy-done = f32[192,512]{1,0:T(8,128)S(1)} copy-done((f32[192,512]{1,0:T(8,128)S(1)}, f32[192,512]{1,0:T(8,128)}, u32[]{:S(2)}) %copy-start) | copy-done | bytes 393240
  1.0 0.5 gram.2
  1.5 13.7 %all_to_all.20.refs_0_ = f32[8,16,1152]{2,1,0:T(8,128)S(1)} all-to-all(f32[8,16,1152]{2,1,0:T(8,128)S(1)} %gram.2), channel_id=1, replica_groups=mesh['pair'=64,'rows'=8] {'rows'}, dimensions={0} | all-to-all | bytes 1179648 | tf_op jit(solution)/shard_map/all_to_all | solution.py:378
  15.2 0.0 copy-start.1
  15.3 10.6 %all_to_all.21.packed_ref = f32[8,16,1152]{2,1,0:T(8,128)S(1)} all-to-all(f32[8,16,1152]{2,1,0:T(8,128)S(1)} %sum.2), channel_id=1, replica_groups=mesh['pair'=64,'rows'=8] {'rows'}, dimensions={0} | all-to-all | bytes 1179648 | tf_op jit(solution)/shard_map/all_to_all | solution.py:388
  25.8 0.0 copy-start.2
  25.8 0.0 copy-done.1
  25.8 0.7 copy-done.2
  26.5 6.5 %polar.2 = (f32[384,256]{1,0:T(8,128)S(1)}, f32[216,256]{1,0:T(8,128)S(1)}) custom-call(s32[2]{0:T(128)S(1)} %bitcast.1, f32[8,16,1152]{2,1,0:T(8,128)S(1)} %all_to_all.21.packed_ref, f32[192,512]{1,0:T(8,128)S(1)} %copy-done.1), custom_call_target="tpu_custom_call" | custom-call | tf_op jit(solution)/shard_map/polar/pallas_call | solution.py:391
  33.0 7.7 %collective-permute-start.1 = (f32[384,256]{1,0:T(8,128)S(1)}, f32[384,256]{1,0:T(8,128)S(1)}, u32[]{:S(2)}, u32[]{:S(2)}) collective-permute-start(f32[384,256]{1,0:T(8,128)S(1)} %get-tuple-element.10), channel_id=1, source_target_pairs={{0,8},{8,0},{16,24},{24,16},{32,40},{40,32},{48,56},{56,48},{64,72... | collective-permute-start | bytes 1179656 | tf_op jit(solution)/shard_map/ppermute | solution.py:19
  40.7 4.4 %collective-permute-start = (f32[216,256]{1,0:T(8,128)S(1)}, f32[216,256]{1,0:T(8,128)S(1)}, u32[]{:S(2)}, u32[]{:S(2)}) collective-permute-start(f32[216,256]{1,0:T(8,128)S(1)} %get-tuple-element.9), channel_id=1, source_target_pairs={{0,504},{8,16},{16,8},{24,32},{32,24},{40,48},{48,40},{56,64},{64,... | collective-permute-start | bytes 663560 | tf_op jit(solution)/shard_map/ppermute | solution.py:25
  45.0 5.2 %collective-permute-done.far_ref.refs_0_.refs_1_ = f32[216,256]{1,0:T(8,128)S(1)} collective-permute-done((f32[216,256]{1,0:T(8,128)S(1)}, f32[216,256]{1,0:T(8,128)S(1)}, u32[]{:S(2)}, u32[]{:S(2)}) %collective-permute-start) | collective-permute-done | bytes 221216 | tf_op jit(solution)/shard_map/ppermute | solution.py:25
  50.3 0.0 collective-permute-done.1.near_ref.refs_0_
  50.3 0.3 gram.3
  50.6 8.2 %all_to_all.22.refs_1_ = f32[8,16,512]{2,1,0:T(8,128)S(1)} all-to-all(f32[8,16,512]{2,1,0:T(8,128)S(1)} %gram.3), channel_id=1, replica_groups=mesh['pair'=64,'rows'=8] {'rows'}, dimensions={0} | all-to-all | bytes 524288 | tf_op jit(solution)/shard_map/all_to_all | solution.py:378
  58.8 10.8 %all_to_all.23.packed_ref = f32[8,16,896]{2,1,0:T(8,128)S(1)} all-to-all(f32[8,16,896]{2,1,0:T(8,128)S(1)} %sum.3), channel_id=1, replica_groups=mesh['pair'=64,'rows'=8] {'rows'}, dimensions={0} | all-to-all | bytes 917504 | tf_op jit(solution)/shard_map/all_to_all | solution.py:388
  69.6 4.3 %polar.3 = (f32[192,256]{1,0:T(8,128)S(1)}, f32[192,256]{1,0:T(8,128)S(1)}) custom-call(s32[2]{0:T(128)S(1)} %bitcast.2, f32[8,16,896]{2,1,0:T(8,128)S(1)} %all_to_all.23.packed_ref, f32[384,256]{1,0:T(8,128)S(1)} %collective-permute-done.1.near_ref.refs_0_, f32[216,256]{1,0:T(8,128)S(1)} %collective-permute-done.far_ref.refs_0_.refs_1_), custom_call_target="tpu_custom_call" | custom-call | tf_op jit(solution)/shard_map/polar/pallas_call | solution.py:391
  74.0 12.3 %collective-permute-start.2 = (f32[192,256]{1,0:T(8,128)S(1)}, f32[192,256]{1,0:T(8,128)S(1)}, u32[]{:S(2)}, u32[]{:S(2)}) collective-permute-start(f32[192,256]{1,0:T(8,128)S(1)} %get-tuple-element.11), channel_id=1, source_target_pairs={{0,8},{8,0},{16,24},{24,16},{32,40},{40,32},{48,56},{56,48},{64,72... | collective-permute-start | bytes 589832 | tf_op jit(solution)/shard_map/ppermute | solution.py:19
  86.3 1.9 %collective-permute-start.3 = (f32[192,256]{1,0:T(8,128)S(1)}, f32[192,256]{1,0:T(8,128)S(1)}, u32[]{:S(2)}, u32[]{:S(2)}) collective-permute-start(f32[192,256]{1,0:T(8,128)S(1)} %get-tuple-element.12), channel_id=1, source_target_pairs={{0,504},{8,16},{16,8},{24,32},{32,24},{40,48},{48,40},{56,64},{64,... | collective-permute-start | bytes 589832 | tf_op jit(solution)/shard_map/ppermute | solution.py:25
  88.2 0.0 collective-permute-done.2.near_ref
  88.3 8.7 %collective-permute-done.3.far_ref = f32[192,256]{1,0:T(8,128)S(1)} collective-permute-done((f32[192,256]{1,0:T(8,128)S(1)}, f32[192,256]{1,0:T(8,128)S(1)}, u32[]{:S(2)}, u32[]{:S(2)}) %collective-permute-start.3) | collective-permute-done | bytes 196640 | tf_op jit(solution)/shard_map/ppermute | solution.py:25
  96.9 0.8 place.1
  (2 shorter events, 0.1 us)
Async XLA Ops:
  0.0 1.0 %copy-start = (f32[192,512]{1,0:T(8,128)S(1)}, f32[192,512]{1,0:T(8,128)}, u32[]{:S(2)}) copy-start(f32[192,512]{1,0:T(8,128)} %refs_0_.3) | copy-start | bytes 1179652
  15.2 10.6 %copy-start.1 = (f32[192,512]{1,0:T(8,128)S(1)}, f32[192,512]{1,0:T(8,128)}, u32[]{:S(2)}) copy-start(f32[192,512]{1,0:T(8,128)} %refs_0_.3) | copy-start | bytes 1179652
  25.8 0.7 copy-start.2
  33.0 17.3 %collective-permute-start.1 = (f32[384,256]{1,0:T(8,128)S(1)}, f32[384,256]{1,0:T(8,128)S(1)}, u32[]{:S(2)}, u32[]{:S(2)}) collective-permute-start(f32[384,256]{1,0:T(8,128)S(1)} %get-tuple-element.10), channel_id=1, source_target_pairs={{0,8},{8,0},{16,24},{24,16},{32,40},{40,32},{48,56},{56,48},{64,72... | collective-permute-start | bytes 1179656 | tf_op jit(solution)/shard_map/ppermute | solution.py:19
  40.7 9.6 %collective-permute-start = (f32[216,256]{1,0:T(8,128)S(1)}, f32[216,256]{1,0:T(8,128)S(1)}, u32[]{:S(2)}, u32[]{:S(2)}) collective-permute-start(f32[216,256]{1,0:T(8,128)S(1)} %get-tuple-element.9), channel_id=1, source_target_pairs={{0,504},{8,16},{16,8},{24,32},{32,24},{40,48},{48,40},{56,64},{64,... | collective-permute-start | bytes 663560 | tf_op jit(solution)/shard_map/ppermute | solution.py:25
  74.0 14.3 %collective-permute-start.2 = (f32[192,256]{1,0:T(8,128)S(1)}, f32[192,256]{1,0:T(8,128)S(1)}, u32[]{:S(2)}, u32[]{:S(2)}) collective-permute-start(f32[192,256]{1,0:T(8,128)S(1)} %get-tuple-element.11), channel_id=1, source_target_pairs={{0,8},{8,0},{16,24},{24,16},{32,40},{40,32},{48,56},{56,48},{64,72... | collective-permute-start | bytes 589832 | tf_op jit(solution)/shard_map/ppermute | solution.py:19
  86.3 10.6 %collective-permute-start.3 = (f32[192,256]{1,0:T(8,128)S(1)}, f32[192,256]{1,0:T(8,128)S(1)}, u32[]{:S(2)}, u32[]{:S(2)}) collective-permute-start(f32[192,256]{1,0:T(8,128)S(1)} %get-tuple-element.12), channel_id=1, source_target_pairs={{0,504},{8,16},{16,8},{24,32},{32,24},{40,48},{48,40},{56,64},{64,... | collective-permute-start | bytes 589832 | tf_op jit(solution)/shard_map/ppermute | solution.py:25

commit v6 on v5

--- a/solution.py
+++ b/solution.py
@@ -136,8 +136,8 @@
         copy.wait()
 
 
-MATRICES = 5
-PAIRS = 7
+MATRICES = 4
+PAIRS = 9
 
 
 def polar_scratch(rows, size):
@@ -154,9 +154,9 @@
     scratch = len(polar_scratch(8, 8))
     *block_refs, near_ref, far_ref = refs[:-scratch]
     refs = refs[-scratch:]
-    dev, two, zed, bee, sqr = refs[:MATRICES]
+    dev, two, zed, bee = refs[:MATRICES]
     pairs = refs[MATRICES : MATRICES + 2 * PAIRS]
-    dev_s, two_s, mix_s, zed_s, dub_s, bee_s, sqr_s = zip(pairs[::2], pairs[1::2])
+    cor_s, dev_s, two_s, mix_s, zed_s, dub_s, bee_s, map_s, way_s = zip(pairs[::2], pairs[1::2])
     val, val_h, val_l, far_diag = refs[MATRICES + 2 * PAIRS :]
     opening, closing = turn == 0, turn == ROUNDS - 1
     parts, part_rows, _ = packed_ref.shape
@@ -192,11 +192,14 @@
             return near[count : count + mid, at(place[1])]
         return jnp.concatenate([near[count + mid :, at(0)], near[count + mid :, at(1)]], axis=0)
 
-    along, down = [], []
-    for i in range(4):
-        total = jnp.sum(jnp.where(eye, gram_at((i, i)), 0.0), axis=0, keepdims=True)
-        along.append(lax.rsqrt(total + EPS * total_rows))
-        down.append(jnp.broadcast_to(along[i], (mid, mid)).T)
+    guard = EPS * total_rows
+    totals = [
+        jnp.sum(jnp.where(eye, gram_at((i, i)), 0.0), axis=0, keepdims=True) for i in range(4)
+    ]
+    share = sum(total / (total + guard) for total in totals)
+    share = jnp.sum(share, axis=1, keepdims=True) / size
+    along = [lax.rsqrt((total + guard) * share) for total in totals]
+    down = [jnp.broadcast_to(line, (mid, mid)).T for line in along]
     square = jnp.zeros((8, mid), jnp.float32)
     square_off = jnp.zeros((8, mid), jnp.float32)
     for i, j in places:
@@ -204,12 +207,17 @@
         term = jnp.sum((corr * corr).reshape(mid // 8, 8, mid), axis=0)
         if i == j:
             square = square + term
+            cor_s[0][at(i), at(i)], cor_s[1][at(i), at(i)] = split(corr)
             corr = corr - one
         else:
             square_off = square_off + term
         for row, column, value in ((i, j, corr),) if i == j else ((i, j, corr), (j, i, corr.T)):
             dev[at(row), at(column)] = value
-            dev_s[0][at(row), at(column)], dev_s[1][at(row), at(column)] = split(value)
+            parted = split(value)
+            for k in range(2):
+                dev_s[k][at(row), at(column)] = parted[k]
+                if i != j and not closing:
+                    cor_s[k][at(row), at(column)] = parted[k]
     square = square + 2.0 * square_off
     square = jnp.sum(jnp.sum(square, axis=0, keepdims=True), axis=1, keepdims=True)
     s = lax.rsqrt(square / size)
@@ -252,17 +260,24 @@
         two[piece, column] = s * value + (s * c_zero * c_zero) * dev[piece, column]
         put_split(dub_s, piece, column, s * value)
 
+    def on_diagonal(piece, column, shape, value):
+        rows = lax.broadcasted_iota(jnp.int32, shape, 0) + piece.start
+        columns = lax.broadcasted_iota(jnp.int32, shape, 1) + column.start
+        return jnp.where(rows == columns, value, 0.0)
+
     def keep_bee(piece, column, value):
-        value = value + two[piece, column]
-        rows = lax.broadcasted_iota(jnp.int32, value.shape, 0) + piece.start
-        columns = lax.broadcasted_iota(jnp.int32, value.shape, 1) + column.start
-        value = value + jnp.where(rows == columns, s * c_zero * c_zero - 1.0, 0.0)
+        shift = on_diagonal(piece, column, value.shape, s * c_zero * c_zero - 1.0)
+        value = value + two[piece, column] + shift
         bee[piece, column] = value
         put_split(bee_s, piece, column, value)
 
-    def keep_sqr(piece, column, value):
-        sqr[piece, column] = value
-        put_split(sqr_s, piece, column, value)
+    def keep_map(piece, column, value):
+        value = zed[piece, column] - 0.5 * (c_zero * bee[piece, column] + value)
+        value = value + on_diagonal(piece, column, value.shape, c_zero)
+        put_split(map_s, piece, column, value)
+
+    def keep_way(piece, column, value):
+        put_split(way_s, piece, column, value)
 
     symmetric(dev_s, dev_s, keep_two, two_s + mix_s)
     symmetric(two_s, mix_s, keep_zed, zed_s)
@@ -283,19 +298,20 @@
         plan = ((zed_s, c_zero), (dev_s, 1.0), (zed_s, c_zero), (zed_s, c_zero))
         mine, other = 1.5 * norm, -0.5 * norm * s
     else:
-        plan = ((zed_s, c_zero), (bee_s, 0.0))
-        mine, other = norm, -0.5 * norm
+        symmetric(zed_s, zed_s, keep_dub, dub_s)
+        symmetric(dev_s, dub_s, keep_bee, bee_s)
+        symmetric(bee_s, zed_s, keep_map, map_s)
+        plan = ((map_s, None),)
     for step, (right, factor) in enumerate(plan):
-        if right is bee_s:
-            symmetric(zed_s, zed_s, keep_dub, dub_s)
-            symmetric(dev_s, dub_s, keep_bee, bee_s)
         new = []
         for column in halves:
             product = times(slice(None), (val_h.at[step], val_l.at[step]), right, column)
 
             def store(piece, value):
-                if right is not bee_s:
-                    value = value + factor * val[step, piece, column]
+                if factor is None:
+                    new.append(norm * value)
+                    return
+                value = value + factor * val[step, piece, column]
                 if step == len(plan) - 1:
                     new.append(mine * val[1, piece, column] + other * value)
                 else:
@@ -310,19 +326,15 @@
         far_ref[piece] = jnp.where(head, new[steps + k], new[k])
     if closing:
         return
-    symmetric(bee_s, bee_s, keep_sqr, sqr_s)
+    symmetric(cor_s, map_s, keep_way, way_s)
     grams = []
     for column in halves:
         gram = []
 
         def keep_gram(piece, value):
-            piece_in = slice(piece.start + column.start, piece.stop + column.start)
-            value = 0.25 * value - 0.75 * sqr[piece_in, column]
-            rows = lax.broadcasted_iota(jnp.int32, value.shape, 0) + piece.start
-            columns = lax.broadcasted_iota(jnp.int32, value.shape, 1)
-            gram.append(total_rows * (value + jnp.where(rows == columns, 1.0, 0.0)))
-
-        put(times(column, sqr_s, bee_s, column), keep_gram)
+            gram.append((total_rows * s) * value)
+
+        put(times(column, map_s, way_s, column), keep_gram)
         grams.append(gram)
     steps = len(grams[0])
     for k in range(steps):

time: 98.1 us -> 98.7 us (level)
  no operation moved by 1% of the time
where the time goes in v6:
time: 98.7 us; the launch traced here: 98.3 us
  blocking collectives  43.2 us (44%)
  starting transfers between devices  26.3 us (27%)
  waiting for transfers between devices  13.9 us (14%)
  Pallas kernels  13.2 us (13%)
  local copies, waits for them, and re-layouts  1.65 us (2%)
    all_to_all x2, blocking collectives, local(): terms = lax.all_to_all(partial, 'rows', 0, 0)  21.9 us
    all_to_all x2, blocking collectives, local(): gathered = lax.all_to_all(summed, 'rows', 0, 0)  21.4 us
    ppermute x2, starting transfers between devices, swapped_near(): return lax.ppermute(value, axis, [(i, i ^ 1) for i in range(count)])  20 us
    ppermute x2, waiting for transfers between devices, swapped_far(): return lax.ppermute(value, axis, pairs)  13.9 us
    pallas_call x2, Pallas kernels, local(): pl.pallas_call(functools.partial(polar_kernel, float(total_rows), turn),...  11.5 us
    ppermute x2, starting transfers between devices, swapped_far(): return lax.ppermute(value, axis, pairs)  6.28 us
  transfers between devices with their start and end apart: 4, of which 2 were waited for; matrix products, arithmetic and copies ran while one was open for 0% of the time, Pallas kernels for 0%

profile of v6, /device:TPU:1, one launch (start us, length us, event | category | flops | bytes accessed | tf_op | source)
XLA Modules:
  0.0 98.3 jit_solution(17380334464544330304)
XLA Ops:
  0.0 0.0 copy-start
  0.0 1.0 %copy-done = f32[192,512]{1,0:T(8,128)S(1)} copy-done((f32[192,512]{1,0:T(8,128)S(1)}, f32[192,512]{1,0:T(8,128)}, u32[]{:S(2)}) %copy-start) | copy-done | bytes 393240
  1.0 0.5 gram.2
  1.5 13.7 %all_to_all.20.refs_0_ = f32[8,16,1152]{2,1,0:T(8,128)S(1)} all-to-all(f32[8,16,1152]{2,1,0:T(8,128)S(1)} %gram.2), channel_id=1, replica_groups=mesh['pair'=64,'rows'=8] {'rows'}, dimensions={0} | all-to-all | bytes 1179648 | tf_op jit(solution)/shard_map/all_to_all | solution.py:390
  15.2 0.0 copy-start.1
  15.3 10.6 %all_to_all.21.packed_ref = f32[8,16,1152]{2,1,0:T(8,128)S(1)} all-to-all(f32[8,16,1152]{2,1,0:T(8,128)S(1)} %sum.2), channel_id=1, replica_groups=mesh['pair'=64,'rows'=8] {'rows'}, dimensions={0} | all-to-all | bytes 1179648 | tf_op jit(solution)/shard_map/all_to_all | solution.py:400
  25.8 0.0 copy-start.2
  25.8 0.0 copy-done.1
  25.8 0.7 copy-done.2
  26.5 7.1 %polar.2 = (f32[384,256]{1,0:T(8,128)S(1)}, f32[216,256]{1,0:T(8,128)S(1)}) custom-call(s32[2]{0:T(128)S(1)} %bitcast.1, f32[8,16,1152]{2,1,0:T(8,128)S(1)} %all_to_all.21.packed_ref, f32[192,512]{1,0:T(8,128)S(1)} %copy-done.1), custom_call_target="tpu_custom_call" | custom-call | tf_op jit(solution)/shard_map/polar/pallas_call | solution.py:403
  33.6 7.7 %collective-permute-start.1 = (f32[384,256]{1,0:T(8,128)S(1)}, f32[384,256]{1,0:T(8,128)S(1)}, u32[]{:S(2)}, u32[]{:S(2)}) collective-permute-start(f32[384,256]{1,0:T(8,128)S(1)} %get-tuple-element.10), channel_id=1, source_target_pairs={{0,8},{8,0},{16,24},{24,16},{32,40},{40,32},{48,56},{56,48},{64,72... | collective-permute-start | bytes 1179656 | tf_op jit(solution)/shard_map/ppermute | solution.py:19
  41.3 4.4 %collective-permute-start = (f32[216,256]{1,0:T(8,128)S(1)}, f32[216,256]{1,0:T(8,128)S(1)}, u32[]{:S(2)}, u32[]{:S(2)}) collective-permute-start(f32[216,256]{1,0:T(8,128)S(1)} %get-tuple-element.9), channel_id=1, source_target_pairs={{0,504},{8,16},{16,8},{24,32},{32,24},{40,48},{48,40},{56,64},{64,... | collective-permute-start | bytes 663560 | tf_op jit(solution)/shard_map/ppermute | solution.py:25
  45.6 5.2 %collective-permute-done.far_ref.refs_0_.refs_1_ = f32[216,256]{1,0:T(8,128)S(1)} collective-permute-done((f32[216,256]{1,0:T(8,128)S(1)}, f32[216,256]{1,0:T(8,128)S(1)}, u32[]{:S(2)}, u32[]{:S(2)}) %collective-permute-start) | collective-permute-done | bytes 221216 | tf_op jit(solution)/shard_map/ppermute | solution.py:25
  50.9 0.0 collective-permute-done.1.near_ref.refs_0_
  50.9 0.3 gram.3
  51.2 8.2 %all_to_all.22.refs_1_ = f32[8,16,512]{2,1,0:T(8,128)S(1)} all-to-all(f32[8,16,512]{2,1,0:T(8,128)S(1)} %gram.3), channel_id=1, replica_groups=mesh['pair'=64,'rows'=8] {'rows'}, dimensions={0} | all-to-all | bytes 524288 | tf_op jit(solution)/shard_map/all_to_all | solution.py:390
  59.4 10.8 %all_to_all.23.packed_ref = f32[8,16,896]{2,1,0:T(8,128)S(1)} all-to-all(f32[8,16,896]{2,1,0:T(8,128)S(1)} %sum.3), channel_id=1, replica_groups=mesh['pair'=64,'rows'=8] {'rows'}, dimensions={0} | all-to-all | bytes 917504 | tf_op jit(solution)/shard_map/all_to_all | solution.py:400
  70.2 4.4 %polar.3 = (f32[192,256]{1,0:T(8,128)S(1)}, f32[192,256]{1,0:T(8,128)S(1)}) custom-call(s32[2]{0:T(128)S(1)} %bitcast.2, f32[8,16,896]{2,1,0:T(8,128)S(1)} %all_to_all.23.packed_ref, f32[384,256]{1,0:T(8,128)S(1)} %collective-permute-done.1.near_ref.refs_0_, f32[216,256]{1,0:T(8,128)S(1)} %collective-permute-done.far_ref.refs_0_.refs_1_), custom_call_target="tpu_custom_call" | custom-call | tf_op jit(solution)/shard_map/polar/pallas_call | solution.py:403
  74.7 12.3 %collective-permute-start.2 = (f32[192,256]{1,0:T(8,128)S(1)}, f32[192,256]{1,0:T(8,128)S(1)}, u32[]{:S(2)}, u32[]{:S(2)}) collective-permute-start(f32[192,256]{1,0:T(8,128)S(1)} %get-tuple-element.11), channel_id=1, source_target_pairs={{0,8},{8,0},{16,24},{24,16},{32,40},{40,32},{48,56},{56,48},{64,72... | collective-permute-start | bytes 589832 | tf_op jit(solution)/shard_map/ppermute | solution.py:19
  87.0 1.9 %collective-permute-start.3 = (f32[192,256]{1,0:T(8,128)S(1)}, f32[192,256]{1,0:T(8,128)S(1)}, u32[]{:S(2)}, u32[]{:S(2)}) collective-permute-start(f32[192,256]{1,0:T(8,128)S(1)} %get-tuple-element.12), channel_id=1, source_target_pairs={{0,504},{8,16},{16,8},{24,32},{32,24},{40,48},{48,40},{56,64},{64,... | collective-permute-start | bytes 589832 | tf_op jit(solution)/shard_map/ppermute | solution.py:25
  88.9 0.0 collective-permute-done.2.near_ref
  88.9 8.7 %collective-permute-done.3.far_ref = f32[192,256]{1,0:T(8,128)S(1)} collective-permute-done((f32[192,256]{1,0:T(8,128)S(1)}, f32[192,256]{1,0:T(8,128)S(1)}, u32[]{:S(2)}, u32[]{:S(2)}) %collective-permute-start.3) | collective-permute-done | bytes 196640 | tf_op jit(solution)/shard_map/ppermute | solution.py:25
  97.6 0.8 place.1
  (2 shorter events, 0.1 us)
Async XLA Ops:
  0.0 1.0 %copy-start = (f32[192,512]{1,0:T(8,128)S(1)}, f32[192,512]{1,0:T(8,128)}, u32[]{:S(2)}) copy-start(f32[192,512]{1,0:T(8,128)} %refs_0_.3) | copy-start | bytes 1179652
  15.2 10.6 %copy-start.1 = (f32[192,512]{1,0:T(8,128)S(1)}, f32[192,512]{1,0:T(8,128)}, u32[]{:S(2)}) copy-start(f32[192,512]{1,0:T(8,128)} %refs_0_.3) | copy-start | bytes 1179652
  25.8 0.7 copy-start.2
  33.6 17.3 %collective-permute-start.1 = (f32[384,256]{1,0:T(8,128)S(1)}, f32[384,256]{1,0:T(8,128)S(1)}, u32[]{:S(2)}, u32[]{:S(2)}) collective-permute-start(f32[384,256]{1,0:T(8,128)S(1)} %get-tuple-element.10), channel_id=1, source_target_pairs={{0,8},{8,0},{16,24},{24,16},{32,40},{40,32},{48,56},{56,48},{64,72... | collective-permute-start | bytes 1179656 | tf_op jit(solution)/shard_map/ppermute | solution.py:19
  41.3 9.6 %collective-permute-start = (f32[216,256]{1,0:T(8,128)S(1)}, f32[216,256]{1,0:T(8,128)S(1)}, u32[]{:S(2)}, u32[]{:S(2)}) collective-permute-start(f32[216,256]{1,0:T(8,128)S(1)} %get-tuple-element.9), channel_id=1, source_target_pairs={{0,504},{8,16},{16,8},{24,32},{32,24},{40,48},{48,40},{56,64},{64,... | collective-permute-start | bytes 663560 | tf_op jit(solution)/shard_map/ppermute | solution.py:25
  74.7 14.3 %collective-permute-start.2 = (f32[192,256]{1,0:T(8,128)S(1)}, f32[192,256]{1,0:T(8,128)S(1)}, u32[]{:S(2)}, u32[]{:S(2)}) collective-permute-start(f32[192,256]{1,0:T(8,128)S(1)} %get-tuple-element.11), channel_id=1, source_target_pairs={{0,8},{8,0},{16,24},{24,16},{32,40},{40,32},{48,56},{56,48},{64,72... | collective-permute-start | bytes 589832 | tf_op jit(solution)/shard_map/ppermute | solution.py:19
  87.0 10.6 %collective-permute-start.3 = (f32[192,256]{1,0:T(8,128)S(1)}, f32[192,256]{1,0:T(8,128)S(1)}, u32[]{:S(2)}, u32[]{:S(2)}) collective-permute-start(f32[192,256]{1,0:T(8,128)S(1)} %get-tuple-element.12), channel_id=1, source_target_pairs={{0,504},{8,16},{16,8},{24,32},{32,24},{40,48},{48,40},{56,64},{64,... | collective-permute-start | bytes 589832 | tf_op jit(solution)/shard_map/ppermute | solution.py:25
